TPU v7x, 256 devices: a whole 4x4x8 slice. The times are simulated.
256 devices in a mesh: build: 2 (over y_lo), test: 8 (over x, core), stmt: 16 (over y_hi, z).
Axes of the slice: x: 4, y: 4 (y_hi: 2, y_lo: 2; y = y_hi * 2 + y_lo), z: 8, core: 2. Of those that a mesh axis runs over, the one named last changes fastest.
Arguments:
- tile_values: bfloat16 [2, 8, 16, 2, 128, 128, 128], P('build', 'test', 'stmt'), may hold values from -6 to 6
- tile_test: int32 [2, 8, 16, 2], P('build', 'test', 'stmt'), may hold values from 0 to 3, as said below
- tile_stmt: int32 [2, 8, 16, 2], P('build', 'test', 'stmt'), may hold values from 0 to 1, as said below
- tile_build: int32 [2, 8, 16, 2], P('build', 'test', 'stmt'), may hold values from 0 to 5, as said below
- tile_count: int32 [2, 8, 16], P('build', 'test', 'stmt'), may hold values from 0 to 2, as said below
- test_factor: bfloat16 [8, 512, 256], P('test', ('build', 'stmt')), may hold values from -0.027063294 to 0.027063294
- build_factor: bfloat16 [2, 768, 256], P('build', ('test', 'stmt')), may hold values from -0.027063294 to 0.027063294
Outputs:
- stmt_factor: float32 [16, 256, 256], P('stmt', ('build', 'test'))
Inputs may be any that keep to these rules, and one draw needn't show every extreme that they name: `tile_count`: slots from this count on hold padding: their values and block numbers must not contribute. Some grid position has every slot live and some has none. `tile_test`: test block of a slot; the largest block is named in every draw. `tile_stmt`: statement block of a slot; the largest block is named in every draw. `tile_build`: build block of a slot; the largest block is named in every draw.
All inputs are finite; a program needn't handle non-finite values.
Results may differ from a plain program's by a relative error of at most 0.003.
Values may be sent and summed in bfloat16 or wider, within the bound.
A program may use at most 64 MiB of HBM per device.

v0:
```python
import jax
import jax.numpy as jnp
from jax import lax
from jax.sharding import Mesh
from jax.sharding import PartitionSpec as P

TILE = 128
SB = 2
BUILD_STMT = ("build", "stmt_0", "stmt_1")
TEST_STMT = ("test_0", "test_1", "stmt_0", "stmt_1")
BUILD_TEST = ("build", "test_0", "test_1")
TEST = ("test_0", "test_1")
STMT = ("stmt_0", "stmt_1")


def copy_for_each(x, axis):
    copies = jnp.broadcast_to(x, (lax.axis_size(axis), *x.shape))
    return lax.all_to_all(copies, axis, split_axis=0, concat_axis=0, tiled=True)


def in_order(pieces, dim):
    pieces = jnp.moveaxis(pieces, 0, dim)
    lengths = pieces.shape
    return pieces.reshape(*lengths[:dim], lengths[dim] * lengths[dim + 1], *lengths[dim + 2 :])


def gather_directly(x, axis, dim):
    pieces = copy_for_each(x, axis)
    return in_order(pieces, dim)


def all_blocks(x, axes, order):
    pieces = x[None]
    for k in order:
        pieces = lax.all_gather(pieces, axes[k], axis=0, tiled=True)
    block = [lax.axis_size(axes[k]) for k in reversed(order)]
    pieces = pieces.reshape(*block, *x.shape)
    turned = sorted(range(len(order)), key=lambda place: order[len(order) - 1 - place])
    return pieces.transpose(*turned, *range(len(order), pieces.ndim)).reshape(-1, *x.shape)


def gathered_by_axis(x, axes, order, dim):
    return in_order(all_blocks(x, axes, order), dim)


def over_copies(x, axis):
    everything = copy_for_each(x, axis)
    return jnp.sum(everything, axis=0)


def shards(tile_values, tile_test, tile_stmt, tile_build, tile_count, test_factor, build_factor):
    test_slab = gather_directly(test_factor, BUILD_STMT, 1)[0]
    build_slab = gathered_by_axis(build_factor, TEST_STMT, (2, 0, 3, 1), 1)[0]
    slot_values = tile_values[0, 0, 0]
    slot_tests = tile_test[0, 0, 0]
    slot_stmts = tile_stmt[0, 0, 0]
    slot_builds = tile_build[0, 0, 0]
    live_count = tile_count[0, 0, 0]
    tile_width = slot_values.shape[-1]
    rank_width = test_slab.shape[1]
    running_sum = jnp.zeros((SB * TILE, rank_width), jnp.float32)
    for slot_index in range(slot_values.shape[0]):
        test_block = lax.dynamic_slice_in_dim(
            test_slab, slot_tests[slot_index] * tile_width, tile_width, 0
        ).astype(jnp.float32)
        build_block = lax.dynamic_slice_in_dim(
            build_slab, slot_builds[slot_index] * tile_width, tile_width, 0
        ).astype(jnp.float32)
        khatri_rao = (test_block[:, None, :] * build_block[None, :, :]).astype(jnp.bfloat16)
        term = jnp.einsum(
            "ijk,ikr->jr", slot_values[slot_index], khatri_rao, preferred_element_type=jnp.float32
        )
        live_weight = (slot_index < live_count).astype(jnp.float32)
        accumulate_term = term * live_weight
        start_row = slot_stmts[slot_index] * tile_width
        current = lax.dynamic_slice_in_dim(running_sum, start_row, tile_width, 0)
        running_sum = lax.dynamic_update_slice_in_dim(
            running_sum, current + accumulate_term, start_row, 0
        )
    owned_sums = lax.psum_scatter(running_sum, BUILD_TEST, scatter_dimension=0, tiled=True)
    slab_test_gram = jnp.dot(test_slab.T, test_slab, preferred_element_type=jnp.float32)
    slab_build_gram = jnp.dot(build_slab.T, build_slab, preferred_element_type=jnp.float32)
    gram_test = over_copies(slab_test_gram, TEST)
    gram_build = over_copies(slab_build_gram, "build")
    gram = gram_test * gram_build
    lower = jnp.linalg.cholesky(gram)
    halfway = lax.linalg.triangular_solve(
        lower, owned_sums, left_side=False, lower=True, transpose_a=True
    )
    solved = lax.linalg.triangular_solve(
        lower, halfway, left_side=False, lower=True, transpose_a=False
    )
    return solved[None]


def solution(mesh):
    torus = Mesh(
        mesh.devices.reshape(mesh.shape["build"], 4, 2, 2, 8),
        ("build", "test_0", "test_1", "stmt_0", "stmt_1"),
    )
    return jax.shard_map(
        shards,
        mesh=torus,
        in_specs=(
            P("build", TEST, STMT, None, None, None, None),
            P("build", TEST, STMT, None),
            P("build", TEST, STMT, None),
            P("build", TEST, STMT, None),
            P("build", TEST, STMT),
            P(TEST, BUILD_STMT, None),
            P("build", TEST_STMT, None),
        ),
        out_specs=P(STMT, BUILD_TEST, None),
        check_vma=False,
    )
```

profile of v0, /device:TPU:1, one launch (start us, length us, event | category | flops | bytes accessed | tf_op | source)
XLA Modules:
  0.0 184.6 jit_solution(16512295211425270760)
XLA Ops:
  6.5 1.4 broadcast_in_dim.25
  8.0 12.0 %all-to-all-start = ((bf16[32,1,16,256]{3,2,1,0:T(8,128)(2,1)}), bf16[32,1,16,256]{3,2,1,0:T(8,128)(2,1)S(1)}, u32[]{:S(2)}, u32[]{:S(2)}) async-start(bf16[32,1,16,256]{3,2,1,0:T(8,128)(2,1)} %broadcast_in_dim.25), calls=%async_computation | async-start | bytes 524288 | tf_op jit(solution)/shard_map/all_to_all | solution.py:18
  20.0 4.8 %all-gather = bf16[2,6,256]{2,1,0:T(8,128)(2,1)S(1)} all-gather(bf16[1,6,256]{2,1,0:T(8,128)(2,1)} %param.13), channel_id=2, replica_groups=mesh['build'=2,'test_0'=4,'test_1'=2,'stmt_0'=2,'stmt_1'=8] {'stmt_0'}, dimensions={0}, use_global_device_ids=true | all-gather | bytes 9216 | tf_op jit(solution)/shard_map/all_gather | solution.py:35
  24.8 9.9 %all-gather.1 = bf16[8,6,256]{2,1,0:T(8,128)(2,1)S(1)} all-gather(bf16[2,6,256]{2,1,0:T(8,128)(2,1)S(1)} %all-gather), channel_id=3, replica_groups=mesh['build'=2,'test_0'=4,'test_1'=2,'stmt_0'=2,'stmt_1'=8] {'test_0'}, dimensions={0}, use_global_device_ids=true | all-gather | bytes 30720 | tf_op jit(solution)/shard_map/all_gather | solution.py:35
  34.7 19.3 %all-gather.2 = bf16[64,6,256]{2,0,1:T(8,128)(2,1)S(1)} all-gather(bf16[8,6,256]{2,0,1:T(8,128)(2,1)S(1)} %copy.29), channel_id=4, replica_groups=mesh['build'=2,'test_0'=4,'test_1'=2,'stmt_0'=2,'stmt_1'=8] {'stmt_1'}, dimensions={0}, use_global_device_ids=true | all-gather | bytes 221184 | tf_op jit(solution)/shard_map/all_gather | solution.py:35
  54.1 12.9 %all-gather.3 = bf16[128,6,256]{2,0,1:T(8,128)(2,1)S(1)} all-gather(bf16[64,6,256]{2,0,1:T(8,128)(2,1)S(1)} %all-gather.2), channel_id=5, replica_groups=mesh['build'=2,'test_0'=4,'test_1'=2,'stmt_0'=2,'stmt_1'=8] {'test_1'}, dimensions={0}, use_global_device_ids=true | all-gather | bytes 589824 | tf_op jit(solution)/shard_map/all_gather | solution.py:35
  66.9 0.2 reshape.73
  67.1 0.3 convolution_bitcast_fusion
  67.5 0.9 broadcast_in_dim.28
  68.4 3.5 %all-to-all-start.2 = ((f32[2,256,256]{2,1,0:T(8,128)}), f32[2,256,256]{2,1,0:T(8,128)S(1)}, u32[]{:S(2)}, u32[]{:S(2)}) async-start(f32[2,256,256]{2,1,0:T(8,128)} %broadcast_in_dim.28), calls=%async_computation.3 | async-start | bytes 1048576 | tf_op jit(solution)/shard_map/all_to_all | solution.py:18
  71.9 0.6 fusion.54
  72.5 0.3 convolution_bitcast_fusion.1
  72.8 6.8 %all-to-all-done.2 = f32[2,256,256]{2,1,0:T(8,128)S(1)} async-done(((f32[2,256,256]{2,1,0:T(8,128)}), f32[2,256,256]{2,1,0:T(8,128)S(1)}, u32[]{:S(2)}, u32[]{:S(2)}) %all-to-all-start.2) | async-done | bytes 524320 | tf_op jit(solution)/shard_map/all_to_all | solution.py:18
  79.6 1.5 broadcast_in_dim.27
  81.1 4.9 %all-to-all-start.1 = ((f32[8,256,256]{2,1,0:T(8,128)}), f32[8,256,256]{2,1,0:T(8,128)S(1)}, u32[]{:S(2)}, u32[]{:S(2)}) async-start(f32[8,256,256]{2,1,0:T(8,128)} %broadcast_in_dim.27), calls=%async_computation.2 | async-start | bytes 4194304 | tf_op jit(solution)/shard_map/all_to_all | solution.py:18
  85.9 0.7 fusion.53
  87.8 0.2 copy.55
  89.5 0.7 fusion.55
  91.5 0.1 squeeze_reshape_transpose_reshape.3
  91.7 0.1 copy.32
  92.6 0.1 copy.38
  92.7 1.0 dynamic-slice_convert_fusion.1
  93.8 8.5 %fusion.28 = f32[256,256]{1,0:T(8,128)S(1)} fusion(f32[256,256]{1,0:T(8,128)S(1)} %broadcast_in_dim.24, s32[]{:T(128)S(6)} %select_n.25, bf16[1,1,1,2,128,128,128]{6,5,4,3,2,1,0:T(8,128)(2,1)} %param.7, f32[128,256]{0,1:T(8,128)S(1)} %copy.32, f32[128,256]{1,0:T(8,128)S(1)} %get-tuple-element.26, f32[]{:T(128)} %bitcast.8), kind=kOutput, calls=%fused_computation.22 | convolution fusion | flops 1082163200 | bytes 4588036 | tf_op jit(solution)/shard_map/ijk,ikr->jr/dot_general | solution.py:70
  102.4 5.3 %fusion.34 = f32[256,256]{1,0:T(8,128)S(1)} fusion(f32[256,256]{1,0:T(8,128)S(1)} %fusion.28, s32[]{:T(128)S(6)} %select_n.26, bf16[1,1,1,2,128,128,128]{6,5,4,3,2,1,0:T(8,128)(2,1)S(1)} %bitcast.125, f32[128,256]{0,1:T(8,128)S(1)} %copy.34, f32[128,256]{1,0:T(8,128)S(1)} %get-tuple-element.25, f32[]{:T(128)} %bitcast.16), kind=kOutput, calls=%fused_computation.24 | convolution fusion | flops 1082195968 | bytes 4718600 | tf_op jit(solution)/shard_map/ijk,ikr->jr/dot_general | solution.py:70
  107.7 0.7 copy-done
  108.4 3.7 %all-to-all-done.1 = f32[8,256,256]{2,1,0:T(8,128)S(1)} async-done(((f32[8,256,256]{2,1,0:T(8,128)}), f32[8,256,256]{2,1,0:T(8,128)S(1)}, u32[]{:S(2)}, u32[]{:S(2)}) %all-to-all-start.1) | async-done | bytes 2097184 | tf_op jit(solution)/shard_map/all_to_all | solution.py:18
  112.1 0.1 reduce_sum.18
  112.3 0.1 copy.37
  112.5 0.1 copy.39
  112.7 11.7 %cholesky.49 = f32[128,128]{1,0:T(8,128)S(1)} custom-call(f32[128,128]{1,0:T(8,128)S(1)} %cholesky.115), custom_call_target="Cholesky" | custom-call | tf_op jit(solution)/shard_map/jit(cholesky)/cholesky | solution.py:86
  124.4 9.8 %custom-call.16 = f32[1,128,128]{1,2,0:T(8,128)S(1)} custom-call(f32[1,128,128]{2,1,0:T(8,128)S(1)} %get-tuple-element.30), custom_call_target="InvertDiagBlocksLowerTriangular" | custom-call | tf_op jit(solution)/shard_map/jit(cholesky)/cholesky | solution.py:86
  134.2 0.2 constant_dynamic-update-slice_fusion
  134.5 0.3 convolution_subtract_fusion
  134.7 11.7 %cholesky.103 = f32[128,128]{1,0:T(8,128)S(1)} custom-call(f32[128,128]{1,0:T(8,128)S(1)} %convolution_subtract_fusion), custom_call_target="Cholesky" | custom-call | tf_op jit(solution)/shard_map/jit(cholesky)/cholesky | solution.py:86
  146.5 0.7 compare_reduce_fusion
  148.6 5.4 %while.1 = (s32[]{:T(128)}, f32[256,256]{1,0:T(8,128)S(1)}, s32[2,2]{1,0:T(2,128)S(1)}, f32[2,128,128]{2,1,0:T(8,128)}, s32[]{:T(128)}) while((s32[]{:T(128)}, f32[256,256]{1,0:T(8,128)S(1)}, s32[2,2]{1,0:T(2,128)S(1)}, f32[2,128,128]{2,1,0:T(8,128)}, s32[]{:T(128)}) %tuple.28), condition=%wide.while_cond, body=%wide.while_body.sunk | while | flops 2 | bytes 132705 | solution.py:87
  148.6 0.7 fusion.64
  149.3 2.0 %bitcast_dynamic-update-slice_fusion.2 = f32[2,128,128]{2,1,0:T(8,128)} fusion(f32[2,128,128]{2,1,0:T(8,128)} %get-tuple-element.78, s32[]{:T(128)} %get-tuple-element.75, f32[256,256]{1,0:T(8,128)S(1)} %get-tuple-element.81, s32[]{:T(128)} %bitcast.119, s32[]{:T(128)} %bitcast.120), kind=kLoop, calls=%fused_computation.clone.1 | loop fusion | bytes 132608 | tf_op jit(solution)/shard_map/triangular_solve
  151.3 0.7 fusion.64
  152.0 2.0 %bitcast_dynamic-update-slice_fusion.2 = f32[2,128,128]{2,1,0:T(8,128)} fusion(f32[2,128,128]{2,1,0:T(8,128)} %get-tuple-element.78, s32[]{:T(128)} %get-tuple-element.75, f32[256,256]{1,0:T(8,128)S(1)} %get-tuple-element.81, s32[]{:T(128)} %bitcast.119, s32[]{:T(128)} %bitcast.120), kind=kLoop, calls=%fused_computation.clone.1 | loop fusion | bytes 132608 | tf_op jit(solution)/shard_map/triangular_solve
  154.0 20.5 %custom-call.17 = f32[2,128,128]{1,2,0:T(8,128)S(1)} custom-call(f32[2,128,128]{2,1,0:T(8,128)} %get-tuple-element.12), custom_call_target="InvertDiagBlocksLowerTriangular" | custom-call | tf_op jit(solution)/shard_map/triangular_solve | solution.py:87
  174.5 0.8 fusion.46
  175.4 0.9 convolution_subtract_fusion.2
  176.2 0.2 fusion.48
  176.4 0.2 fusion.47
  176.6 0.2 convolution_subtract_fusion.1
  176.8 0.2 fusion.45
  177.0 0.7 maximum_bitcast_fusion
  (35 shorter events, 0.5 us)
Async XLA Ops:
  6.5 65.3 %copy-start.2 = (s32[1,1,1,2]{3,2,1,0:T(1,128)S(1)}, s32[1,1,1,2]{3,2,1,0:T(1,128)}, u32[]{:S(2)}) copy-start(s32[1,1,1,2]{3,2,1,0:T(1,128)} %param.10) | copy-start | bytes 28
  8.0 59.5 %all-to-all-start = ((bf16[32,1,16,256]{3,2,1,0:T(8,128)(2,1)}), bf16[32,1,16,256]{3,2,1,0:T(8,128)(2,1)S(1)}, u32[]{:S(2)}, u32[]{:S(2)}) async-start(bf16[32,1,16,256]{3,2,1,0:T(8,128)(2,1)} %broadcast_in_dim.25), calls=%async_computation | async-start | bytes 524288 | tf_op jit(solution)/shard_map/all_to_all | solution.py:18
  67.1 18.8 %copy-start.3 = (s32[1,1,1,2]{3,2,1,0:T(1,128)S(1)}, s32[1,1,1,2]{3,2,1,0:T(1,128)}, u32[]{:S(2)}) copy-start(s32[1,1,1,2]{3,2,1,0:T(1,128)} %param.8) | copy-start | bytes 28
  67.4 22.0 %copy-start.4 = (s32[1,1,1,2]{3,2,1,0:T(1,128)S(1)}, s32[1,1,1,2]{3,2,1,0:T(1,128)}, u32[]{:S(2)}) copy-start(s32[1,1,1,2]{3,2,1,0:T(1,128)} %param.9) | copy-start | bytes 28
  67.5 13.6 %copy-start.1 = (bf16[32,1,16,256]{3,2,1,0:T(8,128)(2,1)}, bf16[32,1,16,256]{3,2,1,0:T(8,128)(2,1)S(1)}, u32[]{:S(2)}) copy-start(bf16[32,1,16,256]{3,2,1,0:T(8,128)(2,1)S(1)} %all-to-all-done) | copy-start | bytes 786436
  68.4 11.2 %all-to-all-start.2 = ((f32[2,256,256]{2,1,0:T(8,128)}), f32[2,256,256]{2,1,0:T(8,128)S(1)}, u32[]{:S(2)}, u32[]{:S(2)}) async-start(f32[2,256,256]{2,1,0:T(8,128)} %broadcast_in_dim.28), calls=%async_computation.3 | async-start | bytes 1048576 | tf_op jit(solution)/shard_map/all_to_all | solution.py:18
  81.1 31.1 %all-to-all-start.1 = ((f32[8,256,256]{2,1,0:T(8,128)}), f32[8,256,256]{2,1,0:T(8,128)S(1)}, u32[]{:S(2)}, u32[]{:S(2)}) async-start(f32[8,256,256]{2,1,0:T(8,128)} %broadcast_in_dim.27), calls=%async_computation.2 | async-start | bytes 4194304 | tf_op jit(solution)/shard_map/all_to_all | solution.py:18
  85.9 88.6 %reduce-scatter.2.cloned.1.call-start = ((), (), s32[]{:S(2)}) async-start(), calls=%async_computation.4 | async-start | bytes 278528 | tf_op jit(solution)/shard_map/reduce_scatter | solution.py:80
  92.7 9.6 %slice-start = ((s8[8388608]{0:T(1024)(128)(4,1)}), s8[4194304]{0:T(1024)(128)(4,1)S(1)}, s32[]{:S(2)}) async-start(s8[8388608]{0:T(1024)(128)(4,1)} %bitcast.124), calls=%async_computation.5 | async-start | bytes 8388608
  93.8 8.6 %slice-start.1 = ((s8[8388608]{0:T(1024)(128)(4,1)}), s8[4194304]{0:T(1024)(128)(4,1)S(1)}, s32[]{:S(2)}) async-start(s8[8388608]{0:T(1024)(128)(4,1)} %bitcast.124), calls=%async_computation.6 | async-start | bytes 8388608
  107.7 0.7 copy-start
Sparse Core Ops, SparseCore 0:
  108.5 61.0 reduce-scatter.1
where the time goes:
time: 185 us
  other arithmetic  56.5 us (31%)
  blocking collectives  46.9 us (25%)
  starting transfers between devices  20.4 us (11%)
  between operations  19.7 us (11%)
  matrix products  17.4 us (9%)
  local copies, waits for them, and re-layouts  13 us (7%)
  waiting for transfers between devices  10.6 us (6%)
    all_gather x4, blocking collectives, all_blocks(): pieces = lax.all_gather(pieces, axes[k], axis=0, tiled=True)  46.9 us
    another operation x6, other arithmetic, shards(): lower = jnp.linalg.cholesky(gram)  34 us
    another operation x3, other arithmetic, shards(): lax.linalg.triangular_solve(lower, owned_sums, left_side=False, lower=Tru...  20.5 us
    all_to_all x3, starting transfers between devices, copy_for_each(): return lax.all_to_all(copies, axis, split_axis=0, concat_axis=0, tiled=True)  20.4 us
    dot_general x2, matrix products, shards(): jnp.einsum('ijk,ikr->jr', slot_values[slot_index], khatri_rao, preferred_...  13.8 us
    all_to_all x3, waiting for transfers between devices, copy_for_each(): return lax.all_to_all(copies, axis, split_axis=0, concat_axis=0, tiled=True)  10.5 us
    another operation x6, local copies, waits for them, and re-layouts  5.38 us
    broadcast_in_dim x3, local copies, waits for them, and re-layouts, copy_for_each(): copies = jnp.broadcast_to(x, (lax.axis_size(axis), *x.shape))  3.84 us
  transfers between devices with their start and end apart: 4, of which 2 were waited for; matrix products, arithmetic and copies ran while one was open for 43% of the time, Pallas kernels for 0%

commit v1 on v0

v1 whole, which is shorter than its diff:
```python
import jax
import jax.numpy as jnp
from jax import lax
from jax.sharding import PartitionSpec as P

TILE = 128
SB = 2
ALL = ("build", "test", "stmt")


def shards(tile_values, tile_test, tile_stmt, tile_build, tile_count, test_factor, build_factor):
    test_rows = test_factor[0]
    build_rows = build_factor[0]
    local_grams = jnp.stack(
        [
            lax.dot_general(test_rows, test_rows, (((0,), (0,)), ((), ())), preferred_element_type=jnp.float32),
            lax.dot_general(build_rows, build_rows, (((0,), (0,)), ((), ())), preferred_element_type=jnp.float32),
        ]
    )
    grams = lax.psum(local_grams, ALL)
    gram = grams[0] * grams[1]
    lower = jnp.linalg.cholesky(gram)

    test_slab = lax.all_gather(test_rows, ("build", "stmt"), axis=0, tiled=True)
    build_slab = lax.all_gather(build_rows, ("test", "stmt"), axis=0, tiled=True)
    slot_values = tile_values[0, 0, 0]
    slot_tests = tile_test[0, 0, 0]
    slot_stmts = tile_stmt[0, 0, 0]
    slot_builds = tile_build[0, 0, 0]
    live_count = tile_count[0, 0, 0]
    tile_width = slot_values.shape[-1]
    rank_width = test_slab.shape[1]
    running_sum = jnp.zeros((SB * TILE, rank_width), jnp.float32)
    for slot_index in range(slot_values.shape[0]):
        test_block = lax.dynamic_slice_in_dim(
            test_slab, slot_tests[slot_index] * tile_width, tile_width, 0
        ).astype(jnp.float32)
        build_block = lax.dynamic_slice_in_dim(
            build_slab, slot_builds[slot_index] * tile_width, tile_width, 0
        ).astype(jnp.float32)
        khatri_rao = (test_block[:, None, :] * build_block[None, :, :]).astype(jnp.bfloat16)
        term = jnp.einsum(
            "ijk,ikr->jr", slot_values[slot_index], khatri_rao, preferred_element_type=jnp.float32
        )
        live_weight = (slot_index < live_count).astype(jnp.float32)
        accumulate_term = term * live_weight
        start_row = slot_stmts[slot_index] * tile_width
        current = lax.dynamic_slice_in_dim(running_sum, start_row, tile_width, 0)
        running_sum = lax.dynamic_update_slice_in_dim(
            running_sum, current + accumulate_term, start_row, 0
        )
    owned_sums = lax.psum_scatter(running_sum, ("build", "test"), scatter_dimension=0, tiled=True)
    halfway = lax.linalg.triangular_solve(
        lower, owned_sums, left_side=False, lower=True, transpose_a=True
    )
    solved = lax.linalg.triangular_solve(
        lower, halfway, left_side=False, lower=True, transpose_a=False
    )
    return solved[None]


def solution(mesh):
    return jax.shard_map(
        shards,
        mesh=mesh,
        in_specs=(
            P("build", "test", "stmt", None, None, None, None),
            P("build", "test", "stmt", None),
            P("build", "test", "stmt", None),
            P("build", "test", "stmt", None),
            P("build", "test", "stmt"),
            P("test", ("build", "stmt"), None),
            P("build", ("test", "stmt"), None),
        ),
        out_specs=P("stmt", ("build", "test"), None),
        check_vma=False,
    )
```

time: 185 us -> 510 us (2.76); the launches traced: 185 us -> 502 us
  blocking collectives: 46.9 us -> 368 us
  starting transfers between devices: 20.4 us -> 0.05 us
  waiting for transfers between devices: 10.6 us -> 26.2 us
    all_gather x4 -> x2, blocking collectives: 46.9 us -> 368 us  [the longest x1 304 us: shards(): lax.all_gather(build_rows, ('test', 'stmt'), axis=0, tiled=True)]
    reduce_scatter x1, waiting for transfers between devices: 0.02 us -> 26.2 us  [shards(): lax.psum_scatter(running_sum, ('build', 'test'), scatter_dimension=0, til...]
    all_to_all x3 -> x0, starting transfers between devices: 20.4 us -> none  [copy_for_each(): return lax.all_to_all(copies, axis, split_axis=0, concat_axis=0, tiled=True)]
    all_to_all x3 -> x0, waiting for transfers between devices: 10.5 us -> none  [copy_for_each(): return lax.all_to_all(copies, axis, split_axis=0, concat_axis=0, tiled=True)]
  transfers between devices with their start and end apart: 4 -> 2, of which waited for: 2 -> 1; matrix products, arithmetic and copies ran while one was open for 43% -> 16% of each run, Pallas kernels for 0% -> 0%
where the time goes in v1:
time: 510 us; the launch traced here: 502 us
  blocking collectives  368 us (72%)
  other arithmetic  57.8 us (11%)
  waiting for transfers between devices  26.2 us (5%)
  between operations  20.7 us (4%)
  matrix products  19.4 us (4%)
  local copies, waits for them, and re-layouts  9.57 us (2%)
    all_gather x1, blocking collectives, shards(): lax.all_gather(build_rows, ('test', 'stmt'), axis=0, tiled=True)  304 us
    all_gather x1, blocking collectives, shards(): test_slab = lax.all_gather(test_rows, ('build', 'stmt'), axis=0, tiled=True)  64.6 us
    another operation x6, other arithmetic, shards(): lower = jnp.linalg.cholesky(gram)  34 us
    reduce_scatter x1, waiting for transfers between devices, shards(): lax.psum_scatter(running_sum, ('build', 'test'), scatter_dimension=0, til...  26.2 us
    another operation x3, other arithmetic, shards(): lax.linalg.triangular_solve(lower, owned_sums, left_side=False, lower=Tru...  19.9 us
    dot_general x2, matrix products, shards(): jnp.einsum('ijk,ikr->jr', slot_values[slot_index], khatri_rao, preferred_...  14.4 us
  transfers between devices with their start and end apart: 2, of which 1 were waited for; matrix products, arithmetic and copies ran while one was open for 16% of the time, Pallas kernels for 0%

profile of v1, /device:TPU:1, one launch (start us, length us, event | category | flops | bytes accessed | tf_op | source)
XLA Modules:
  0.0 502.2 jit_solution(10829243908084318337)
XLA Ops:
  7.4 0.0 all-reduce.3.cloned.1.call-start
  7.4 1.0 convolution_bitcast_fusion
  8.4 1.0 convolution_bitcast_fusion.1
  9.4 0.8 pad_maximum_fusion
  10.2 0.0 all-reduce.3.cloned.1.call-update
  10.2 0.0 reduce-scatter.2.cloned.1.call-start
  10.3 1.3 fusion.53
  12.9 0.7 copy.15
  13.6 1.3 fusion.52
  16.2 64.6 %all-gather = bf16[1,512,256]{2,1,0:T(8,128)(2,1)S(1)} all-gather(bf16[1,16,256]{2,1,0:T(8,128)(2,1)} %param.12), channel_id=2, replica_groups=mesh['build'=2,'test'=8,'stmt'=16] {'build','stmt'}, dimensions={1}, use_global_device_ids=true | all-gather | bytes 270336 | tf_op jit(solution)/shard_map/all_gather | solution.py:24
  80.8 1.3 fusion.54
  83.4 303.7 %all-gather.1 = bf16[1,768,256]{2,0,1:T(2,128)(2,1)S(1)} all-gather(bf16[1,6,256]{2,0,1:T(2,128)(2,1)S(1)} %copy.15), channel_id=3, replica_groups=mesh['build'=2,'test'=8,'stmt'=16] {'test','stmt'}, dimensions={1}, use_global_device_ids=true | all-gather | bytes 396288 | tf_op jit(solution)/shard_map/all_gather | solution.py:25
  387.1 0.3 dynamic-slice_convert_fusion
  387.4 0.1 copy.27
  388.2 0.1 copy.29
  388.3 0.0 slice-start
  388.4 0.0 slice-start.1
  388.4 9.1 %fusion.28 = f32[256,256]{1,0:T(8,128)S(1)} fusion(f32[256,256]{1,0:T(8,128)S(1)} %broadcast_in_dim.6, s32[]{:T(128)S(6)} %select_n.25, bf16[1,1,1,2,128,128,128]{6,5,4,3,2,1,0:T(8,128)(2,1)} %param.7, f32[128,256]{0,1:T(8,128)S(1)} %bitcast.119, f32[128,256]{1,0:T(8,128)S(1)} %get-tuple-element.26, f32[]{:T(128)} %bitcast.6), kind=kOutput, calls=%fused_computation.22 | convolution fusion | flops 1082163200 | bytes 4588036 | tf_op jit(solution)/shard_map/ijk,ikr->jr/dot_general | solution.py:42
  397.5 0.0 slice-done
  397.5 0.0 slice-done.1
  397.5 5.3 %fusion.34 = f32[256,256]{1,0:T(8,128)S(1)} fusion(f32[256,256]{1,0:T(8,128)S(1)} %fusion.28, s32[]{:T(128)S(6)} %select_n.26, bf16[1,1,1,2,128,128,128]{6,5,4,3,2,1,0:T(8,128)(2,1)S(1)} %bitcast.122, f32[128,256]{0,1:T(8,128)S(1)} %bitcast.120, f32[128,256]{1,0:T(8,128)S(1)} %get-tuple-element.25, f32[]{:T(128)} %bitcast.16), kind=kOutput, calls=%fused_computation.24 | convolution fusion | flops 1082195968 | bytes 4718600 | tf_op jit(solution)/shard_map/ijk,ikr->jr/dot_general | solution.py:42
  402.8 0.7 copy-done
  403.5 0.0 reduce-scatter.2.cloned.1.call-update
  403.6 0.0 all-reduce.3.cloned.1.call-done
  403.6 1.1 fusion.38
  404.6 0.1 copy.22
  404.8 1.1 fusion.37
  405.9 11.7 %cholesky.49 = f32[128,128]{1,0:T(8,128)S(1)} custom-call(f32[128,128]{1,0:T(8,128)S(1)} %cholesky.115), custom_call_target="Cholesky" | custom-call | tf_op jit(solution)/shard_map/jit(cholesky)/cholesky | solution.py:22
  417.7 9.8 %custom-call.16 = f32[1,128,128]{1,2,0:T(8,128)S(1)} custom-call(f32[1,128,128]{2,1,0:T(8,128)S(1)} %get-tuple-element.30), custom_call_target="InvertDiagBlocksLowerTriangular" | custom-call | tf_op jit(solution)/shard_map/jit(cholesky)/cholesky | solution.py:22
  427.5 0.2 constant_dynamic-update-slice_fusion
  427.7 0.3 convolution_subtract_fusion
  427.9 11.7 %cholesky.103 = f32[128,128]{1,0:T(8,128)S(1)} custom-call(f32[128,128]{1,0:T(8,128)S(1)} %convolution_subtract_fusion), custom_call_target="Cholesky" | custom-call | tf_op jit(solution)/shard_map/jit(cholesky)/cholesky | solution.py:22
  439.7 0.7 compare_reduce_fusion
  441.6 0.1 triangular_solve.67
  441.6 3.8 while.1
  441.7 0.6 fusion.63
  442.2 1.3 bitcast_dynamic-update-slice_fusion.2
  443.5 0.6 fusion.63
  444.1 1.3 bitcast_dynamic-update-slice_fusion.2
  445.4 19.9 %custom-call.17 = f32[2,128,128]{1,2,0:T(8,128)S(1)} custom-call(f32[2,128,128]{2,1,0:T(8,128)S(1)} %get-tuple-element.12), custom_call_target="InvertDiagBlocksLowerTriangular" | custom-call | tf_op jit(solution)/shard_map/triangular_solve | solution.py:53
  465.3 26.2 %reduce-scatter.2.cloned.1.call-done = f32[16,256]{1,0:T(8,128)} async-done(((f32[256,256]{1,0:T(8,128)}), f32[16,256]{1,0:T(8,128)}) %reduce-scatter.2.cloned.1.call-update) | async-done | bytes 16400 | tf_op jit(solution)/shard_map/reduce_scatter | solution.py:52
  491.5 0.8 fusion.43
  492.4 0.9 convolution_subtract_fusion.2
  493.2 0.2 fusion.45
  493.4 0.2 fusion.44
  493.6 0.2 convolution_subtract_fusion.1
  493.8 0.2 fusion.42
  494.0 0.7 maximum_bitcast_fusion
  (13 shorter events, 0.2 us)
Async XLA Ops:
  7.4 396.2 %all-reduce.3.cloned.1.call-start = ((), (), s32[]{:S(2)}) async-start(), calls=%async_computation.2 | async-start | bytes 1048576 | tf_op jit(solution)/shard_map/psum | solution.py:20
  10.2 481.3 %reduce-scatter.2.cloned.1.call-start = ((), (), s32[]{:S(2)}) async-start(), calls=%async_computation.1 | async-start | bytes 278528 | tf_op jit(solution)/shard_map/reduce_scatter | solution.py:52
  388.3 9.2 %slice-start = ((s8[8388608]{0:T(1024)(128)(4,1)}), s8[4194304]{0:T(1024)(128)(4,1)S(1)}, s32[]{:S(2)}) async-start(s8[8388608]{0:T(1024)(128)(4,1)} %bitcast.121), calls=%async_computation.3 | async-start | bytes 8388608
  388.4 9.2 %slice-start.1 = ((s8[8388608]{0:T(1024)(128)(4,1)}), s8[4194304]{0:T(1024)(128)(4,1)S(1)}, s32[]{:S(2)}) async-start(s8[8388608]{0:T(1024)(128)(4,1)} %bitcast.121), calls=%async_computation.4 | async-start | bytes 8388608
  402.8 0.7 copy-start
Sparse Core Ops, SparseCore 0:
  13.6 258.6 all-reduce.2
Sparse Core Ops, SparseCore 1:
  403.6 87.8 reduce-scatter.1

commit v2 on v1

--- a/solution.py
+++ b/solution.py
@@ -1,28 +1,129 @@
+import functools
+
 import jax
 import jax.numpy as jnp
 from jax import lax
+from jax.experimental import pallas as pl
+from jax.experimental.pallas import tpu as pltpu
 from jax.sharding import PartitionSpec as P
 
 TILE = 128
 SB = 2
-ALL = ("build", "test", "stmt")
+MESH = pl.DeviceIdType.MESH
+
+
+def gather_kernel(n_build, n_test, n_stmt, test_in, build_in, test_out, build_out,
+                  test_scr, build_scr, test_send, test_recv, build_send, build_recv):
+    b = lax.axis_index("build")
+    t = lax.axis_index("test")
+    s = lax.axis_index("stmt")
+    my_p = b * n_stmt + s
+    my_q = t * n_stmt + s
+
+    def test_out_copy(p):
+        return pltpu.make_async_remote_copy(
+            src_ref=test_in, dst_ref=test_scr.at[my_p], send_sem=test_send.at[p],
+            recv_sem=test_recv.at[my_p], device_id=(p // n_stmt, t, p % n_stmt),
+            device_id_type=MESH)
+
+    def test_in_copy(p):
+        return pltpu.make_async_remote_copy(
+            src_ref=test_in, dst_ref=test_scr.at[p], send_sem=test_send.at[p],
+            recv_sem=test_recv.at[p], device_id=(p // n_stmt, t, p % n_stmt),
+            device_id_type=MESH)
+
+    def build_out_copy(q):
+        return pltpu.make_async_remote_copy(
+            src_ref=build_in, dst_ref=build_scr.at[my_q], send_sem=build_send.at[q],
+            recv_sem=build_recv.at[my_q], device_id=(b, q // n_stmt, q % n_stmt),
+            device_id_type=MESH)
+
+    def build_in_copy(q):
+        return pltpu.make_async_remote_copy(
+            src_ref=build_in, dst_ref=build_scr.at[q], send_sem=build_send.at[q],
+            recv_sem=build_recv.at[q], device_id=(b, q // n_stmt, q % n_stmt),
+            device_id_type=MESH)
+
+    def start_test(p, carry):
+        @pl.when(p != my_p)
+        def _():
+            test_out_copy(p).start()
+        return carry
+
+    def start_build(q, carry):
+        @pl.when(q != my_q)
+        def _():
+            build_out_copy(q).start()
+        return carry
+
+    lax.fori_loop(0, n_build * n_stmt, start_test, 0)
+    lax.fori_loop(0, n_test * n_stmt, start_build, 0)
+    test_scr[pl.ds(my_p, 1)] = test_in[...][None]
+    build_scr[pl.ds(my_q, 1)] = build_in[...][None]
+
+    def wait_test(p, carry):
+        @pl.when(p != my_p)
+        def _():
+            test_out_copy(p).wait_send()
+            test_in_copy(p).wait_recv()
+        return carry
+
+    def wait_build(q, carry):
+        @pl.when(q != my_q)
+        def _():
+            build_out_copy(q).wait_send()
+            build_in_copy(q).wait_recv()
+        return carry
+
+    lax.fori_loop(0, n_build * n_stmt, wait_test, 0)
+    lax.fori_loop(0, n_test * n_stmt, wait_build, 0)
+    test_out[...] = test_scr[...]
+    build_out[...] = build_scr[...]
+
+
+def gather_factors(test_rows, build_rows):
+    n_build = lax.axis_size("build")
+    n_test = lax.axis_size("test")
+    n_stmt = lax.axis_size("stmt")
+    n_p = n_build * n_stmt
+    n_q = n_test * n_stmt
+    vmem = pl.BlockSpec(memory_space=pltpu.VMEM)
+    test_pieces, build_pieces = pl.pallas_call(
+        functools.partial(gather_kernel, n_build, n_test, n_stmt),
+        out_shape=(
+            jax.ShapeDtypeStruct((n_p, *test_rows.shape), test_rows.dtype),
+            jax.ShapeDtypeStruct((n_q, *build_rows.shape), build_rows.dtype),
+        ),
+        in_specs=[vmem, vmem],
+        out_specs=(vmem, vmem),
+        scratch_shapes=[
+            pltpu.VMEM((n_p, *test_rows.shape), test_rows.dtype),
+            pltpu.VMEM((n_q, *build_rows.shape), build_rows.dtype),
+            pltpu.SemaphoreType.DMA((n_p,)),
+            pltpu.SemaphoreType.DMA((n_p,)),
+            pltpu.SemaphoreType.DMA((n_q,)),
+            pltpu.SemaphoreType.DMA((n_q,)),
+        ],
+        compiler_params=pltpu.CompilerParams(has_side_effects=True),
+    )(test_rows, build_rows)
+    return (
+        test_pieces.reshape(-1, test_rows.shape[-1]),
+        build_pieces.reshape(-1, build_rows.shape[-1]),
+    )
+
+
+def copy_for_each(x, axis):
+    copies = jnp.broadcast_to(x, (lax.axis_size(axis), *x.shape))
+    return lax.all_to_all(copies, axis, split_axis=0, concat_axis=0, tiled=True)
+
+
+def over_copies(x, axis):
+    everything = copy_for_each(x, axis)
+    return jnp.sum(everything, axis=0)
 
 
 def shards(tile_values, tile_test, tile_stmt, tile_build, tile_count, test_factor, build_factor):
-    test_rows = test_factor[0]
-    build_rows = build_factor[0]
-    local_grams = jnp.stack(
-        [
-            lax.dot_general(test_rows, test_rows, (((0,), (0,)), ((), ())), preferred_element_type=jnp.float32),
-            lax.dot_general(build_rows, build_rows, (((0,), (0,)), ((), ())), preferred_element_type=jnp.float32),
-        ]
-    )
-    grams = lax.psum(local_grams, ALL)
-    gram = grams[0] * grams[1]
-    lower = jnp.linalg.cholesky(gram)
-
-    test_slab = lax.all_gather(test_rows, ("build", "stmt"), axis=0, tiled=True)
-    build_slab = lax.all_gather(build_rows, ("test", "stmt"), axis=0, tiled=True)
+    test_slab, build_slab = gather_factors(test_factor[0], build_factor[0])
     slot_values = tile_values[0, 0, 0]
     slot_tests = tile_test[0, 0, 0]
     slot_stmts = tile_stmt[0, 0, 0]
@@ -50,6 +151,12 @@
             running_sum, current + accumulate_term, start_row, 0
         )
     owned_sums = lax.psum_scatter(running_sum, ("build", "test"), scatter_dimension=0, tiled=True)
+    slab_test_gram = jnp.dot(test_slab.T, test_slab, preferred_element_type=jnp.float32)
+    slab_build_gram = jnp.dot(build_slab.T, build_slab, preferred_element_type=jnp.float32)
+    gram_test = over_copies(slab_test_gram, "test")
+    gram_build = over_copies(slab_build_gram, "build")
+    gram = gram_test * gram_build
+    lower = jnp.linalg.cholesky(gram)
     halfway = lax.linalg.triangular_solve(
         lower, owned_sums, left_side=False, lower=True, transpose_a=True
     )

time: 510 us -> 169 us (0.33); the launches traced: 502 us -> 168 us
  blocking collectives: 368 us -> 0 us
  Pallas kernels: 0 us -> 38.4 us
  waiting for transfers between devices: 26.2 us -> 9.42 us
  starting transfers between devices: 0.05 us -> 14.7 us
    all_gather x2 -> x0, blocking collectives: 368 us -> none  [the longest x1 304 us: shards(): lax.all_gather(build_rows, ('test', 'stmt'), axis=0, tiled=True)]
    pallas_call x0 -> x1, Pallas kernels: none -> 38.4 us  [gather_factors(): pl.pallas_call(functools.partial(gather_kernel, n_build, n_test, n_stmt),...]
    reduce_scatter x1, waiting for transfers between devices: 26.2 us -> 0.02 us  [shards(): lax.psum_scatter(running_sum, ('build', 'test'), scatter_dimension=0, til...]
    all_to_all x0 -> x2, starting transfers between devices: none -> 14.7 us  [copy_for_each(): return lax.all_to_all(copies, axis, split_axis=0, concat_axis=0, tiled=True)]
    all_to_all x0 -> x2, waiting for transfers between devices: none -> 9.39 us  [copy_for_each(): return lax.all_to_all(copies, axis, split_axis=0, concat_axis=0, tiled=True)]
  transfers between devices with their start and end apart: 2 -> 3, of which waited for: 1 -> 2; matrix products, arithmetic and copies ran while one was open for 16% -> 47% of each run, Pallas kernels for 0% -> 0%
where the time goes in v2:
time: 169 us; the launch traced here: 168 us
  other arithmetic  55.9 us (33%)
  Pallas kernels  38.4 us (23%)
  matrix products  19.7 us (12%)
  between operations  19.4 us (11%)
  starting transfers between devices  14.7 us (9%)
  local copies, waits for them, and re-layouts  10.6 us (6%)
  waiting for transfers between devices  9.42 us (6%)
    pallas_call x1, Pallas kernels, gather_factors(): pl.pallas_call(functools.partial(gather_kernel, n_build, n_test, n_stmt),...  38.4 us
    another operation x6, other arithmetic, shards(): lower = jnp.linalg.cholesky(gram)  34 us
    another operation x3, other arithmetic, shards(): lax.linalg.triangular_solve(lower, owned_sums, left_side=False, lower=Tru...  19.9 us
    all_to_all x2, starting transfers between devices, copy_for_each(): return lax.all_to_all(copies, axis, split_axis=0, concat_axis=0, tiled=True)  14.7 us
    dot_general x2, matrix products, shards(): jnp.einsum('ijk,ikr->jr', slot_values[slot_index], khatri_rao, preferred_...  13.8 us
    all_to_all x2, waiting for transfers between devices, copy_for_each(): return lax.all_to_all(copies, axis, split_axis=0, concat_axis=0, tiled=True)  9.39 us
    another operation x6, local copies, waits for them, and re-layouts  4.02 us
  transfers between devices with their start and end apart: 3, of which 2 were waited for; matrix products, arithmetic and copies ran while one was open for 47% of the time, Pallas kernels for 0%

profile of v2, /device:TPU:1, one launch (start us, length us, event | category | flops | bytes accessed | tf_op | source)
XLA Modules:
  0.0 168.1 jit_solution(18250968824106398416)
XLA Ops:
  6.5 38.4 %shard_map.73 = (bf16[32,16,256]{2,1,0:T(8,128)(2,1)}, bf16[128,6,256]{2,1,0:T(8,128)(2,1)}) custom-call(bf16[16,256]{1,0:T(8,128)(2,1)} %bitcast.108, bf16[6,256]{1,0:T(8,128)(2,1)} %bitcast.109), custom_call_target="tpu_custom_call" | custom-call | tf_op jit(solution)/shard_map/pallas_call | solution.py:91
  44.9 1.6 convolution_bitcast_fusion
  46.5 0.8 broadcast_in_dim.20
  47.3 3.5 %all-to-all-start.1 = ((f32[2,256,256]{2,1,0:T(8,128)}), f32[2,256,256]{2,1,0:T(8,128)S(1)}, u32[]{:S(2)}, u32[]{:S(2)}) async-start(f32[2,256,256]{2,1,0:T(8,128)} %broadcast_in_dim.20), calls=%async_computation.2 | async-start | bytes 1048576 | tf_op jit(solution)/shard_map/all_to_all | solution.py:117
  50.8 1.3 fusion.50
  52.2 1.3 convolution_bitcast_fusion.1
  53.5 5.2 %all-to-all-done.1 = f32[2,256,256]{2,1,0:T(8,128)S(1)} async-done(((f32[2,256,256]{2,1,0:T(8,128)}), f32[2,256,256]{2,1,0:T(8,128)S(1)}, u32[]{:S(2)}, u32[]{:S(2)}) %all-to-all-start.1) | async-done | bytes 524320 | tf_op jit(solution)/shard_map/all_to_all | solution.py:117
  58.7 1.5 broadcast_in_dim.19
  60.2 11.2 %all-to-all-start = ((f32[8,256,256]{2,1,0:T(8,128)}), f32[8,256,256]{2,1,0:T(8,128)S(1)}, u32[]{:S(2)}, u32[]{:S(2)}) async-start(f32[8,256,256]{2,1,0:T(8,128)} %broadcast_in_dim.19), calls=%async_computation.1 | async-start | bytes 4194304 | tf_op jit(solution)/shard_map/all_to_all | solution.py:117
  71.5 0.7 fusion.52
  74.7 0.0 copy-done.3
  74.7 0.7 fusion.51
  76.6 0.1 reshape.68
  77.4 0.1 copy.28
  77.5 0.1 copy.26
  77.6 0.0 slice-start
  77.7 1.0 dynamic-slice_convert_fusion.1
  78.7 0.0 slice-start.1
  78.8 8.5 %fusion.28 = f32[256,256]{1,0:T(8,128)S(1)} fusion(f32[256,256]{1,0:T(8,128)S(1)} %broadcast_in_dim.18, s32[]{:T(128)S(6)} %select_n.25, bf16[1,1,1,2,128,128,128]{6,5,4,3,2,1,0:T(8,128)(2,1)} %param.7, f32[128,256]{0,1:T(8,128)S(1)} %copy.26, f32[128,256]{1,0:T(8,128)S(1)} %get-tuple-element.30, f32[]{:T(128)} %bitcast.7), kind=kOutput, calls=%fused_computation.22 | convolution fusion | flops 1082163200 | bytes 4588036 | tf_op jit(solution)/shard_map/ijk,ikr->jr/dot_general | solution.py:143
  87.3 5.3 %fusion.34 = f32[256,256]{1,0:T(8,128)S(1)} fusion(f32[256,256]{1,0:T(8,128)S(1)} %fusion.28, s32[]{:T(128)S(6)} %select_n.26, bf16[1,1,1,2,128,128,128]{6,5,4,3,2,1,0:T(8,128)(2,1)S(1)} %bitcast.111, f32[128,256]{0,1:T(8,128)S(1)} %copy.28, f32[128,256]{1,0:T(8,128)S(1)} %get-tuple-element.29, f32[]{:T(128)} %bitcast.15), kind=kOutput, calls=%fused_computation.24 | convolution fusion | flops 1082195968 | bytes 4718600 | tf_op jit(solution)/shard_map/ijk,ikr->jr/dot_general | solution.py:143
  92.6 0.7 copy-done
  93.3 0.0 reduce-scatter.2.cloned.1.call-update
  93.4 0.1 copy.33
  93.5 4.1 %all-to-all-done = f32[8,256,256]{2,1,0:T(8,128)S(1)} async-done(((f32[8,256,256]{2,1,0:T(8,128)}), f32[8,256,256]{2,1,0:T(8,128)S(1)}, u32[]{:S(2)}, u32[]{:S(2)}) %all-to-all-start) | async-done | bytes 2097184 | tf_op jit(solution)/shard_map/all_to_all | solution.py:117
  97.7 0.1 reduce_sum.18
  97.8 0.1 copy.32
  98.0 0.1 copy.34
  98.2 11.7 %cholesky.49 = f32[128,128]{1,0:T(8,128)S(1)} custom-call(f32[128,128]{1,0:T(8,128)S(1)} %cholesky.115), custom_call_target="Cholesky" | custom-call | tf_op jit(solution)/shard_map/jit(cholesky)/cholesky | solution.py:159
  110.0 9.8 %custom-call.16 = f32[1,128,128]{1,2,0:T(8,128)S(1)} custom-call(f32[1,128,128]{2,1,0:T(8,128)S(1)} %get-tuple-element.34), custom_call_target="InvertDiagBlocksLowerTriangular" | custom-call | tf_op jit(solution)/shard_map/jit(cholesky)/cholesky | solution.py:159
  119.8 0.2 constant_dynamic-update-slice_fusion
  120.0 0.3 convolution_subtract_fusion
  120.2 11.7 %cholesky.103 = f32[128,128]{1,0:T(8,128)S(1)} custom-call(f32[128,128]{1,0:T(8,128)S(1)} %convolution_subtract_fusion), custom_call_target="Cholesky" | custom-call | tf_op jit(solution)/shard_map/jit(cholesky)/cholesky | solution.py:159
  132.0 0.7 compare_reduce_fusion
  134.0 0.1 triangular_solve.67
  134.1 4.1 %while.1 = (s32[]{:T(128)}, f32[256,256]{1,0:T(8,128)S(1)}, s32[2,2]{1,0:T(2,128)S(1)}, f32[2,128,128]{2,1,0:T(8,128)S(1)}, s32[]{:T(128)}) while((s32[]{:T(128)}, f32[256,256]{1,0:T(8,128)S(1)}, s32[2,2]{1,0:T(2,128)S(1)}, f32[2,128,128]{2,1,0:T(8,128)S(1)}, s32[]{:T(128)}) %tuple.28), condition=%wide.while_cond, body=%wide.while_body.sunk | while | flops 2 | bytes 131189 | solution.py:160
  134.1 0.7 fusion.63
  134.8 1.3 bitcast_dynamic-update-slice_fusion.2
  136.1 0.7 fusion.63
  136.8 1.3 bitcast_dynamic-update-slice_fusion.2
  138.1 19.9 %custom-call.17 = f32[2,128,128]{1,2,0:T(8,128)S(1)} custom-call(f32[2,128,128]{2,1,0:T(8,128)S(1)} %get-tuple-element.16), custom_call_target="InvertDiagBlocksLowerTriangular" | custom-call | tf_op jit(solution)/shard_map/triangular_solve | solution.py:160
  158.0 0.0 reduce-scatter.2.cloned.1.call-done
  158.1 0.8 fusion.43
  158.9 0.9 convolution_subtract_fusion.2
  159.8 0.2 fusion.45
  160.0 0.2 fusion.44
  160.2 0.2 convolution_subtract_fusion.1
  160.4 0.2 fusion.42
  160.6 0.7 maximum_bitcast_fusion
  (24 shorter events, 0.3 us)
Async XLA Ops:
  6.5 64.9 %copy-start.2 = (s32[1,1,1,2]{3,2,1,0:T(1,128)S(1)}, s32[1,1,1,2]{3,2,1,0:T(1,128)}, u32[]{:S(2)}) copy-start(s32[1,1,1,2]{3,2,1,0:T(1,128)} %param.9) | copy-start | bytes 28
  6.5 68.1 %copy-start.3 = (s32[1,1,1,2]{3,2,1,0:T(1,128)S(1)}, s32[1,1,1,2]{3,2,1,0:T(1,128)}, u32[]{:S(2)}) copy-start(s32[1,1,1,2]{3,2,1,0:T(1,128)} %param.10) | copy-start | bytes 28
  44.9 31.7 %copy-start.1 = (bf16[128,6,256]{2,1,0:T(8,128)(2,1)S(1)}, bf16[128,6,256]{2,1,0:T(8,128)(2,1)}, u32[]{:S(2)}) copy-start(bf16[128,6,256]{2,1,0:T(8,128)(2,1)} %get-tuple-element.8) | copy-start | bytes 1179652
  47.3 11.4 %all-to-all-start.1 = ((f32[2,256,256]{2,1,0:T(8,128)}), f32[2,256,256]{2,1,0:T(8,128)S(1)}, u32[]{:S(2)}, u32[]{:S(2)}) async-start(f32[2,256,256]{2,1,0:T(8,128)} %broadcast_in_dim.20), calls=%async_computation.2 | async-start | bytes 1048576 | tf_op jit(solution)/shard_map/all_to_all | solution.py:117
  60.2 37.4 %all-to-all-start = ((f32[8,256,256]{2,1,0:T(8,128)}), f32[8,256,256]{2,1,0:T(8,128)S(1)}, u32[]{:S(2)}, u32[]{:S(2)}) async-start(f32[8,256,256]{2,1,0:T(8,128)} %broadcast_in_dim.19), calls=%async_computation.1 | async-start | bytes 4194304 | tf_op jit(solution)/shard_map/all_to_all | solution.py:117
  71.5 86.6 %reduce-scatter.2.cloned.1.call-start = ((), (), s32[]{:S(2)}) async-start(), calls=%async_computation.3 | async-start | bytes 278528 | tf_op jit(solution)/shard_map/reduce_scatter | solution.py:153
  77.6 9.6 %slice-start = ((s8[8388608]{0:T(1024)(128)(4,1)}), s8[4194304]{0:T(1024)(128)(4,1)S(1)}, s32[]{:S(2)}) async-start(s8[8388608]{0:T(1024)(128)(4,1)} %bitcast.110), calls=%async_computation.4 | async-start | bytes 8388608
  78.7 8.6 %slice-start.1 = ((s8[8388608]{0:T(1024)(128)(4,1)}), s8[4194304]{0:T(1024)(128)(4,1)S(1)}, s32[]{:S(2)}) async-start(s8[8388608]{0:T(1024)(128)(4,1)} %bitcast.110), calls=%async_computation.5 | async-start | bytes 8388608
  92.6 0.7 copy-start
Sparse Core Ops, SparseCore 0:
  93.4 57.2 reduce-scatter.1

commit v3 on v2

--- a/solution.py
+++ b/solution.py
@@ -110,6 +110,36 @@
         test_pieces.reshape(-1, test_rows.shape[-1]),
         build_pieces.reshape(-1, build_rows.shape[-1]),
     )
+
+
+def sweep_kernel(g_ref, out_ref):
+    n = g_ref.shape[0]
+    out_ref[...] = g_ref[...]
+    lane = lax.broadcasted_iota(jnp.int32, (1, n), 1)
+
+    def step(k, carry):
+        row = out_ref[pl.ds(k, 1), :]
+        is_k = lane == k
+        pivot = jnp.sum(jnp.where(is_k, row, 0.0), axis=1, keepdims=True)
+        inv = 1.0 / pivot
+        scaled = jnp.where(is_k, 1.0 - inv, row * inv)
+        column = jnp.transpose(jnp.broadcast_to(row, (8, n)))[:, 0:1]
+        out_ref[...] = out_ref[...] - column * scaled
+        out_ref[pl.ds(k, 1), :] = jnp.where(is_k, -inv, row * inv)
+        return carry
+
+    lax.fori_loop(0, n, step, 0)
+    out_ref[...] = -out_ref[...]
+
+
+def spd_inverse(gram):
+    vmem = pl.BlockSpec(memory_space=pltpu.VMEM)
+    return pl.pallas_call(
+        sweep_kernel,
+        out_shape=jax.ShapeDtypeStruct(gram.shape, jnp.float32),
+        in_specs=[vmem],
+        out_specs=vmem,
+    )(gram)
 
 
 def copy_for_each(x, axis):
@@ -156,13 +186,8 @@
     gram_test = over_copies(slab_test_gram, "test")
     gram_build = over_copies(slab_build_gram, "build")
     gram = gram_test * gram_build
-    lower = jnp.linalg.cholesky(gram)
-    halfway = lax.linalg.triangular_solve(
-        lower, owned_sums, left_side=False, lower=True, transpose_a=True
-    )
-    solved = lax.linalg.triangular_solve(
-        lower, halfway, left_side=False, lower=True, transpose_a=False
-    )
+    inverse = spd_inverse(gram)
+    solved = jnp.dot(owned_sums, inverse, precision=lax.Precision.HIGHEST, preferred_element_type=jnp.float32)
     return solved[None]
 
 

time: 169 us -> 166 us (0.982)
  other arithmetic: 55.9 us -> 1.84 us
  Pallas kernels: 38.4 us -> 92 us
  waiting for transfers between devices: 9.42 us -> 12 us
  local copies, waits for them, and re-layouts: 10.6 us -> 8.5 us
  matrix products: 19.7 us -> 18 us
    another operation x9 -> x0, other arithmetic: 54 us -> none  [the longest x6 34 us: shards(): lower = jnp.linalg.cholesky(gram)]
    pallas_call x0 -> x1, Pallas kernels: none -> 53.6 us  [spd_inverse(): pl.pallas_call(sweep_kernel, out_shape=jax.ShapeDtypeStruct(gram.shape, j...]
    another operation x9 -> x0, local copies, waits for them, and re-layouts: 4.12 us -> none
    another operation x8 -> x0, matrix products: 3.01 us -> none  [the longest x3 1.94 us: shards(): lax.linalg.triangular_solve(lower, owned_sums, left_side=False, lower=Tru...]
    all_to_all x2, waiting for transfers between devices: 9.39 us -> 12 us  [copy_for_each(): return lax.all_to_all(copies, axis, split_axis=0, concat_axis=0, tiled=True)]
    dot_general x0 -> x1, matrix products: none -> 1.8 us  [shards(): jnp.dot(owned_sums, inverse, precision=lax.Precision.HIGHEST, preferred_e...]
  transfers between devices with their start and end apart: 3 -> 3, of which waited for: 2 -> 1; matrix products, arithmetic and copies ran while one was open for 47% -> 14% of each run, Pallas kernels for 0% -> 32%
where the time goes in v3:
time: 166 us
  Pallas kernels  92 us (55%)
  matrix products  18 us (11%)
  between operations  18 us (11%)
  starting transfers between devices  15.2 us (9%)
  waiting for transfers between devices  12 us (7%)
  local copies, waits for them, and re-layouts  8.5 us (5%)
  other arithmetic  1.84 us (1%)
    pallas_call x1, Pallas kernels, spd_inverse(): pl.pallas_call(sweep_kernel, out_shape=jax.ShapeDtypeStruct(gram.shape, j...  53.6 us
    pallas_call x1, Pallas kernels, gather_factors(): pl.pallas_call(functools.partial(gather_kernel, n_build, n_test, n_stmt),...  38.4 us
    all_to_all x2, starting transfers between devices, copy_for_each(): return lax.all_to_all(copies, axis, split_axis=0, concat_axis=0, tiled=True)  15.2 us
    dot_general x2, matrix products, shards(): jnp.einsum('ijk,ikr->jr', slot_values[slot_index], khatri_rao, preferred_...  13.4 us
    all_to_all x2, waiting for transfers between devices, copy_for_each(): return lax.all_to_all(copies, axis, split_axis=0, concat_axis=0, tiled=True)  12 us
  transfers between devices with their start and end apart: 3, of which 1 were waited for; matrix products, arithmetic and copies ran while one was open for 14% of the time, Pallas kernels for 32%

profile of v3, /device:TPU:1, one launch (start us, length us, event | category | flops | bytes accessed | tf_op | source)
XLA Modules:
  0.0 165.5 jit_solution(10346042307311180160)
XLA Ops:
  6.5 38.4 %shard_map.73 = (bf16[32,16,256]{2,1,0:T(8,128)(2,1)}, bf16[128,6,256]{2,1,0:T(8,128)(2,1)}) custom-call(bf16[16,256]{1,0:T(8,128)(2,1)} %bitcast.75, bf16[6,256]{1,0:T(8,128)(2,1)} %bitcast.76), custom_call_target="tpu_custom_call" | custom-call | tf_op jit(solution)/shard_map/pallas_call | solution.py:91
  44.9 1.6 convolution_bitcast_fusion
  46.5 0.8 broadcast_in_dim.18
  47.3 3.5 %all-to-all-start.1 = ((f32[2,256,256]{2,1,0:T(8,128)}), f32[2,256,256]{2,1,0:T(8,128)S(1)}, u32[]{:S(2)}, u32[]{:S(2)}) async-start(f32[2,256,256]{2,1,0:T(8,128)} %broadcast_in_dim.18), calls=%async_computation.1 | async-start | bytes 1048576 | tf_op jit(solution)/shard_map/all_to_all | solution.py:147
  50.8 1.3 fusion.38
  53.3 1.3 fusion.39
  56.0 1.2 reshape.47
  57.2 0.9 dynamic-slice_convert_fusion.1
  58.1 1.3 fusion.40
  61.4 0.1 copy.15
  61.5 0.1 copy.14
  61.6 1.3 convolution_bitcast_fusion.1
  62.9 0.0 all-to-all-done.1
  62.9 1.5 broadcast_in_dim.17
  64.4 11.7 %all-to-all-start = ((f32[8,256,256]{2,1,0:T(8,128)}), f32[8,256,256]{2,1,0:T(8,128)S(1)}, u32[]{:S(2)}, u32[]{:S(2)}) async-start(f32[8,256,256]{2,1,0:T(8,128)} %broadcast_in_dim.17), calls=%async_computation | async-start | bytes 4194304 | tf_op jit(solution)/shard_map/all_to_all | solution.py:147
  76.1 0.0 reduce-scatter.4.cloned.1.call-start
  76.1 6.7 %fusion.28 = f32[256,256]{0,1:T(8,128)S(1)} fusion(f32[256,256]{0,1:T(8,128)S(1)} %broadcast_in_dim.16, s32[]{:T(128)S(6)} %select_n.21, bf16[1,1,1,2,128,128,128]{6,5,4,3,2,1,0:T(8,128)(2,1)} %param.7, f32[128,256]{0,1:T(8,128)S(1)} %copy.14, f32[128,256]{1,0:T(8,128)S(1)} %get-tuple-element.12, f32[]{:T(128)} %bitcast.7), kind=kOutput, calls=%fused_computation.20 | convolution fusion | flops 1082163200 | bytes 4588036 | tf_op jit(solution)/shard_map/ijk,ikr->jr/dot_general | solution.py:173
  82.8 6.7 %fusion.34 = f32[256,256]{0,1:T(8,128)S(1)} fusion(f32[256,256]{0,1:T(8,128)S(1)} %fusion.28, s32[]{:T(128)S(6)} %select_n.22, bf16[1,1,1,2,128,128,128]{6,5,4,3,2,1,0:T(8,128)(2,1)} %param.7, f32[128,256]{0,1:T(8,128)S(1)} %copy.15, f32[128,256]{1,0:T(8,128)S(1)} %get-tuple-element.11, f32[]{:T(128)} %bitcast.15), kind=kOutput, calls=%fused_computation.22 | convolution fusion | flops 1082195968 | bytes 4719108 | tf_op jit(solution)/shard_map/ijk,ikr->jr/dot_general | solution.py:173
  89.5 0.8 copy.18
  90.4 0.0 reduce-scatter.4.cloned.1.call-update
  90.4 12.0 %all-to-all-done = f32[8,256,256]{2,1,0:T(8,128)S(1)} async-done(((f32[8,256,256]{2,1,0:T(8,128)}), f32[8,256,256]{2,1,0:T(8,128)S(1)}, u32[]{:S(2)}, u32[]{:S(2)}) %all-to-all-start) | async-done | bytes 2097184 | tf_op jit(solution)/shard_map/all_to_all | solution.py:147
  102.4 0.1 reduce_sum.18
  102.5 0.7 mul.107.g_ref
  103.3 53.6 %shard_map.74 = f32[256,256]{1,0:T(8,128)} custom-call(f32[256,256]{1,0:T(8,128)} %mul.107.g_ref), custom_call_target="tpu_custom_call" | custom-call | tf_op jit(solution)/shard_map/pallas_call | solution.py:137
  156.9 0.0 reduce-scatter.4.cloned.1.call-done
  156.9 1.8 %convolution_bitcast_fusion.2 = f32[1,16,256]{2,1,0:T(8,128)} fusion(f32[16,256]{1,0:T(8,128)} %reduce-scatter.4.cloned.1.call-done, f32[256,256]{1,0:T(8,128)} %shard_map.74), kind=kOutput, calls=%fused_computation.23 | convolution fusion | flops 12582912 | bytes 294912 | tf_op jit(solution)/shard_map/dot_general | solution.py:190
  (3 shorter events, 0.1 us)
Async XLA Ops:
  47.3 15.6 %all-to-all-start.1 = ((f32[2,256,256]{2,1,0:T(8,128)}), f32[2,256,256]{2,1,0:T(8,128)S(1)}, u32[]{:S(2)}, u32[]{:S(2)}) async-start(f32[2,256,256]{2,1,0:T(8,128)} %broadcast_in_dim.18), calls=%async_computation.1 | async-start | bytes 1048576 | tf_op jit(solution)/shard_map/all_to_all | solution.py:147
  64.4 38.0 %all-to-all-start = ((f32[8,256,256]{2,1,0:T(8,128)}), f32[8,256,256]{2,1,0:T(8,128)S(1)}, u32[]{:S(2)}, u32[]{:S(2)}) async-start(f32[8,256,256]{2,1,0:T(8,128)} %broadcast_in_dim.17), calls=%async_computation | async-start | bytes 4194304 | tf_op jit(solution)/shard_map/all_to_all | solution.py:147
  76.1 80.8 %reduce-scatter.4.cloned.1.call-start = ((), (), s32[]{:S(2)}) async-start(), calls=%async_computation.3 | async-start | bytes 278528
Sparse Core Ops, SparseCore 0:
  90.5 56.8 reduce-scatter.3

commit v4 on v3

--- a/solution.py
+++ b/solution.py
@@ -10,6 +10,7 @@
 TILE = 128
 SB = 2
 MESH = pl.DeviceIdType.MESH
+CHUNK = 32
 
 
 def gather_kernel(n_build, n_test, n_stmt, test_in, build_in, test_out, build_out,
@@ -117,18 +118,22 @@
     out_ref[...] = g_ref[...]
     lane = lax.broadcasted_iota(jnp.int32, (1, n), 1)
 
-    def step(k, carry):
-        row = out_ref[pl.ds(k, 1), :]
+    def step(k, row):
         is_k = lane == k
         pivot = jnp.sum(jnp.where(is_k, row, 0.0), axis=1, keepdims=True)
         inv = 1.0 / pivot
         scaled = jnp.where(is_k, 1.0 - inv, row * inv)
-        column = jnp.transpose(jnp.broadcast_to(row, (8, n)))[:, 0:1]
-        out_ref[...] = out_ref[...] - column * scaled
+        column = jnp.transpose(jnp.broadcast_to(row, (TILE, n)))
+        following = jnp.minimum(k + 1, n - 1)
+        next_factor = jnp.sum(jnp.where(lane == following, row, 0.0), axis=1, keepdims=True)
+        next_row = out_ref[pl.ds(following, 1), :] - next_factor * scaled
+        for h in range(n // TILE):
+            lanes = slice(h * TILE, (h + 1) * TILE)
+            out_ref[:, lanes] = out_ref[:, lanes] - column * scaled[:, lanes]
         out_ref[pl.ds(k, 1), :] = jnp.where(is_k, -inv, row * inv)
-        return carry
-
-    lax.fori_loop(0, n, step, 0)
+        return next_row
+
+    lax.fori_loop(0, n, step, out_ref[0:1, :], unroll=4)
     out_ref[...] = -out_ref[...]
 
 
@@ -142,6 +147,59 @@
     )(gram)
 
 
+def mttkrp_kernel(chunk, slot_info, test_ref, build_ref, tile_ref, out_ref, acc_ref):
+    q = pl.program_id(0)
+    c = pl.program_id(1)
+    n_chunks = pl.num_programs(1)
+
+    @pl.when((q == 0) & (c == 0))
+    def _():
+        out_ref[...] = jnp.zeros_like(out_ref)
+
+    @pl.when(c == 0)
+    def _():
+        acc_ref[...] = jnp.zeros_like(acc_ref)
+
+    live = q < slot_info[6]
+
+    @pl.when(live)
+    def _():
+        build_block = build_ref[...].astype(jnp.float32)
+        total = acc_ref[...]
+        for i in range(chunk):
+            test_row = test_ref[i : i + 1, :].astype(jnp.float32)
+            khatri_rao = (test_row * build_block).astype(jnp.bfloat16)
+            total = total + jnp.dot(tile_ref[i], khatri_rao, preferred_element_type=jnp.float32)
+        acc_ref[...] = total
+
+    @pl.when(live & (c == n_chunks - 1))
+    def _():
+        rows = pl.ds(pl.multiple_of(slot_info[4 + q] * TILE, TILE), TILE)
+        out_ref[rows, :] += acc_ref[...]
+
+
+def local_mttkrp(slot_values, slot_info, test_slab, build_slab):
+    slots, width = slot_values.shape[0], slot_values.shape[1]
+    rank = test_slab.shape[1]
+    per_block = width // CHUNK
+    grid_spec = pltpu.PrefetchScalarGridSpec(
+        num_scalar_prefetch=1,
+        grid=(slots, per_block),
+        in_specs=[
+            pl.BlockSpec((CHUNK, rank), lambda q, c, info: (info[q] * per_block + c, 0)),
+            pl.BlockSpec((width, rank), lambda q, c, info: (info[2 + q], 0)),
+            pl.BlockSpec((None, CHUNK, width, width), lambda q, c, info: (q, c, 0, 0)),
+        ],
+        out_specs=pl.BlockSpec((SB * width, rank), lambda q, c, info: (0, 0)),
+        scratch_shapes=[pltpu.VMEM((width, rank), jnp.float32)],
+    )
+    return pl.pallas_call(
+        functools.partial(mttkrp_kernel, CHUNK),
+        out_shape=jax.ShapeDtypeStruct((SB * width, rank), jnp.float32),
+        grid_spec=grid_spec,
+    )(slot_info, test_slab, build_slab, slot_values)
+
+
 def copy_for_each(x, axis):
     copies = jnp.broadcast_to(x, (lax.axis_size(axis), *x.shape))
     return lax.all_to_all(copies, axis, split_axis=0, concat_axis=0, tiled=True)
@@ -155,31 +213,14 @@
 def shards(tile_values, tile_test, tile_stmt, tile_build, tile_count, test_factor, build_factor):
     test_slab, build_slab = gather_factors(test_factor[0], build_factor[0])
     slot_values = tile_values[0, 0, 0]
-    slot_tests = tile_test[0, 0, 0]
-    slot_stmts = tile_stmt[0, 0, 0]
-    slot_builds = tile_build[0, 0, 0]
-    live_count = tile_count[0, 0, 0]
     tile_width = slot_values.shape[-1]
-    rank_width = test_slab.shape[1]
-    running_sum = jnp.zeros((SB * TILE, rank_width), jnp.float32)
-    for slot_index in range(slot_values.shape[0]):
-        test_block = lax.dynamic_slice_in_dim(
-            test_slab, slot_tests[slot_index] * tile_width, tile_width, 0
-        ).astype(jnp.float32)
-        build_block = lax.dynamic_slice_in_dim(
-            build_slab, slot_builds[slot_index] * tile_width, tile_width, 0
-        ).astype(jnp.float32)
-        khatri_rao = (test_block[:, None, :] * build_block[None, :, :]).astype(jnp.bfloat16)
-        term = jnp.einsum(
-            "ijk,ikr->jr", slot_values[slot_index], khatri_rao, preferred_element_type=jnp.float32
-        )
-        live_weight = (slot_index < live_count).astype(jnp.float32)
-        accumulate_term = term * live_weight
-        start_row = slot_stmts[slot_index] * tile_width
-        current = lax.dynamic_slice_in_dim(running_sum, start_row, tile_width, 0)
-        running_sum = lax.dynamic_update_slice_in_dim(
-            running_sum, current + accumulate_term, start_row, 0
-        )
+    slot_info = jnp.concatenate([
+        jnp.clip(tile_test[0, 0, 0], 0, test_slab.shape[0] // tile_width - 1),
+        jnp.clip(tile_build[0, 0, 0], 0, build_slab.shape[0] // tile_width - 1),
+        jnp.clip(tile_stmt[0, 0, 0], 0, SB - 1),
+        tile_count[0, 0, 0][None],
+    ]).astype(jnp.int32)
+    running_sum = local_mttkrp(slot_values, slot_info, test_slab, build_slab)
     owned_sums = lax.psum_scatter(running_sum, ("build", "test"), scatter_dimension=0, tiled=True)
     slab_test_gram = jnp.dot(test_slab.T, test_slab, preferred_element_type=jnp.float32)
     slab_build_gram = jnp.dot(build_slab.T, build_slab, preferred_element_type=jnp.float32)

time: 166 us -> 152 us (0.916)
  waiting for transfers between devices: 12 us -> 34.2 us
  matrix products: 18 us -> 3.61 us
  Pallas kernels: 92 us -> 78.4 us
  local copies, waits for them, and re-layouts: 8.5 us -> 3.23 us
  between operations: 18 us -> 14.2 us
    pallas_call x1, Pallas kernels: 53.6 us -> 33 us  [spd_inverse(): pl.pallas_call(sweep_kernel, out_shape=jax.ShapeDtypeStruct(gram.shape, j...]
    dot_general x2 -> x0, matrix products: 13.4 us -> none  [shards(): jnp.einsum('ijk,ikr->jr', slot_values[slot_index], khatri_rao, preferred_...]
    all_to_all x2, waiting for transfers between devices: 12 us -> 24.5 us  [copy_for_each(): return lax.all_to_all(copies, axis, split_axis=0, concat_axis=0, tiled=True)]
    reduce_scatter x0 -> x1, waiting for transfers between devices: none -> 9.67 us  [shards(): lax.psum_scatter(running_sum, ('build', 'test'), scatter_dimension=0, til...]
    pallas_call x0 -> x1, Pallas kernels: none -> 7.01 us  [local_mttkrp(): pl.pallas_call(functools.partial(mttkrp_kernel, CHUNK), out_shape=jax.Sha...]
    slice x3 -> x0, local copies, waits for them, and re-layouts: 3.94 us -> none  [the longest x1 1.31 us: shards(): slot_tests[slot_index] * tile_width]
  transfers between devices with their start and end apart: 3 -> 3, of which waited for: 1 -> 3; matrix products, arithmetic and copies ran while one was open for 14% -> 2% of each run, Pallas kernels for 32% -> 27%
where the time goes in v4:
time: 152 us; the launch traced here: 150 us
  Pallas kernels  78.4 us (52%)
  waiting for transfers between devices  34.2 us (23%)
  starting transfers between devices  14.8 us (10%)
  between operations  14.2 us (9%)
  matrix products  3.61 us (2%)
  local copies, waits for them, and re-layouts  3.23 us (2%)
  other arithmetic  1.59 us (1%)
    pallas_call x1, Pallas kernels, gather_factors(): pl.pallas_call(functools.partial(gather_kernel, n_build, n_test, n_stmt),...  38.4 us
    pallas_call x1, Pallas kernels, spd_inverse(): pl.pallas_call(sweep_kernel, out_shape=jax.ShapeDtypeStruct(gram.shape, j...  33 us
    all_to_all x2, waiting for transfers between devices, copy_for_each(): return lax.all_to_all(copies, axis, split_axis=0, concat_axis=0, tiled=True)  24.5 us
    all_to_all x2, starting transfers between devices, copy_for_each(): return lax.all_to_all(copies, axis, split_axis=0, concat_axis=0, tiled=True)  14.8 us
    reduce_scatter x1, waiting for transfers between devices, shards(): lax.psum_scatter(running_sum, ('build', 'test'), scatter_dimension=0, til...  9.67 us
    pallas_call x1, Pallas kernels, local_mttkrp(): pl.pallas_call(functools.partial(mttkrp_kernel, CHUNK), out_shape=jax.Sha...  7.01 us
  transfers between devices with their start and end apart: 3, of which 3 were waited for; matrix products, arithmetic and copies ran while one was open for 2% of the time, Pallas kernels for 27%

profile of v4, /device:TPU:1, one launch (start us, length us, event | category | flops | bytes accessed | tf_op | source)
XLA Modules:
  0.0 150.1 jit_solution(5902662882443612065)
XLA Ops:
  6.5 38.4 %shard_map.73 = (bf16[32,16,256]{2,1,0:T(8,128)(2,1)}, bf16[128,6,256]{2,1,0:T(8,128)(2,1)}) custom-call(bf16[16,256]{1,0:T(8,128)(2,1)} %bitcast.24, bf16[6,256]{1,0:T(8,128)(2,1)} %bitcast.25), custom_call_target="tpu_custom_call" | custom-call | tf_op jit(solution)/shard_map/pallas_call | solution.py:92
  44.9 0.0 copy-start.1
  44.9 1.5 %convolution_bitcast_fusion = f32[256,256]{1,0:T(8,128)S(1)} fusion(bf16[128,6,256]{2,1,0:T(8,128)(2,1)} %get-tuple-element.8), kind=kOutput, calls=%fused_computation | convolution fusion | flops 100663296 | bytes 655360 | tf_op jit(solution)/shard_map/dot_general | solution.py:226
  46.5 0.8 broadcast_in_dim.10
  47.3 3.5 %all-to-all-start.1 = ((f32[2,256,256]{2,1,0:T(8,128)}), f32[2,256,256]{2,1,0:T(8,128)S(1)}, u32[]{:S(2)}, u32[]{:S(2)}) async-start(f32[2,256,256]{2,1,0:T(8,128)} %broadcast_in_dim.10), calls=%async_computation.2 | async-start | bytes 1048576 | tf_op jit(solution)/shard_map/all_to_all | solution.py:205
  50.8 0.0 copy-done.1
  50.8 0.3 convolution_bitcast_fusion.1
  51.1 7.6 %all-to-all-done.1 = f32[2,256,256]{2,1,0:T(8,128)S(1)} async-done(((f32[2,256,256]{2,1,0:T(8,128)}), f32[2,256,256]{2,1,0:T(8,128)S(1)}, u32[]{:S(2)}, u32[]{:S(2)}) %all-to-all-start.1) | async-done | bytes 524320 | tf_op jit(solution)/shard_map/all_to_all | solution.py:205
  58.7 1.5 %broadcast_in_dim.9 = f32[8,256,256]{2,1,0:T(8,128)} broadcast(f32[256,256]{1,0:T(8,128)S(1)} %convolution_bitcast_fusion.1), dimensions={1,2} | broadcast | bytes 2359296 | tf_op jit(solution)/shard_map/broadcast_in_dim | solution.py:204
  60.2 0.0 copy-start
  60.2 0.0 copy-start.4
  60.2 0.0 copy-start.2
  60.2 0.0 copy-start.3
  60.2 11.4 %all-to-all-start = ((f32[8,256,256]{2,1,0:T(8,128)}), f32[8,256,256]{2,1,0:T(8,128)S(1)}, u32[]{:S(2)}, u32[]{:S(2)}) async-start(f32[8,256,256]{2,1,0:T(8,128)} %broadcast_in_dim.9), calls=%async_computation.1 | async-start | bytes 4194304 | tf_op jit(solution)/shard_map/all_to_all | solution.py:205
  71.6 0.0 reduce-scatter.2.cloned.1.call-start
  71.6 0.0 copy-done
  71.6 0.9 reshape.16.build_ref
  73.1 0.0 copy-done.4
  73.1 0.0 copy-done.2
  73.1 0.0 copy-done.3
  73.2 0.7 pad_add_fusion.slot_info
  73.8 7.0 %shard_map.74 = f32[256,256]{1,0:T(8,128)} custom-call(s32[7]{0:T(128)} %pad_add_fusion.slot_info, bf16[512,256]{1,0:T(8,128)(2,1)} %bitcast.23, bf16[768,256]{1,0:T(8,128)(2,1)} %reshape.16.build_ref, bf16[2,128,128,128]{3,2,1,0:T(8,128)(2,1)} %bitcast.22), custom_call_target="tpu_custom_call" | custom-call | tf_op jit(solution)/shard_map/pallas_call | solution.py:196
  80.8 0.0 reduce-scatter.2.cloned.1.call-update
  80.9 17.0 %all-to-all-done = f32[8,256,256]{2,1,0:T(8,128)S(1)} async-done(((f32[8,256,256]{2,1,0:T(8,128)}), f32[8,256,256]{2,1,0:T(8,128)S(1)}, u32[]{:S(2)}, u32[]{:S(2)}) %all-to-all-start) | async-done | bytes 2097184 | tf_op jit(solution)/shard_map/all_to_all | solution.py:205
  97.9 0.1 reduce_sum.18
  98.0 0.7 mul.3.g_ref
  98.7 33.0 %shard_map.75 = f32[256,256]{1,0:T(8,128)} custom-call(f32[256,256]{1,0:T(8,128)} %mul.3.g_ref), custom_call_target="tpu_custom_call" | custom-call | tf_op jit(solution)/shard_map/pallas_call | solution.py:142
  131.8 9.7 %reduce-scatter.2.cloned.1.call-done = f32[16,256]{1,0:T(8,128)} async-done(((f32[256,256]{1,0:T(8,128)}), f32[16,256]{1,0:T(8,128)}) %reduce-scatter.2.cloned.1.call-update) | async-done | bytes 16400 | tf_op jit(solution)/shard_map/reduce_scatter | solution.py:224
  141.4 1.8 %convolution_bitcast_fusion.2 = f32[1,16,256]{2,1,0:T(8,128)} fusion(f32[16,256]{1,0:T(8,128)} %reduce-scatter.2.cloned.1.call-done, f32[256,256]{1,0:T(8,128)} %shard_map.75), kind=kOutput, calls=%fused_computation.2 | convolution fusion | flops 12582912 | bytes 294912 | tf_op jit(solution)/shard_map/dot_general | solution.py:231
  (3 shorter events, 0.0 us)
Async XLA Ops:
  44.9 5.9 %copy-start.1 = (bf16[32,16,256]{2,1,0:T(8,128)(2,1)S(1)}, bf16[32,16,256]{2,1,0:T(8,128)(2,1)}, u32[]{:S(2)}) copy-start(bf16[32,16,256]{2,1,0:T(8,128)(2,1)} %get-tuple-element.7) | copy-start | bytes 786436
  47.3 11.4 %all-to-all-start.1 = ((f32[2,256,256]{2,1,0:T(8,128)}), f32[2,256,256]{2,1,0:T(8,128)S(1)}, u32[]{:S(2)}, u32[]{:S(2)}) async-start(f32[2,256,256]{2,1,0:T(8,128)} %broadcast_in_dim.10), calls=%async_computation.2 | async-start | bytes 1048576 | tf_op jit(solution)/shard_map/all_to_all | solution.py:205
  60.2 11.4 %copy-start = (bf16[128,6,256]{2,1,0:T(8,128)(2,1)S(1)}, bf16[128,6,256]{2,1,0:T(8,128)(2,1)}, u32[]{:S(2)}) copy-start(bf16[128,6,256]{2,1,0:T(8,128)(2,1)} %get-tuple-element.8) | copy-start | bytes 1179652
  60.2 12.9 %copy-start.4 = (s32[1,1,1,2]{3,2,1,0:T(1,128)S(1)}, s32[1,1,1,2]{3,2,1,0:T(1,128)}, u32[]{:S(2)}) copy-start(s32[1,1,1,2]{3,2,1,0:T(1,128)} %param.8) | copy-start | bytes 28
  60.2 12.9 %copy-start.2 = (s32[1,1,1,2]{3,2,1,0:T(1,128)S(1)}, s32[1,1,1,2]{3,2,1,0:T(1,128)}, u32[]{:S(2)}) copy-start(s32[1,1,1,2]{3,2,1,0:T(1,128)} %param.9) | copy-start | bytes 28
  60.2 12.9 %copy-start.3 = (s32[1,1,1,2]{3,2,1,0:T(1,128)S(1)}, s32[1,1,1,2]{3,2,1,0:T(1,128)}, u32[]{:S(2)}) copy-start(s32[1,1,1,2]{3,2,1,0:T(1,128)} %param.10) | copy-start | bytes 28
  60.2 37.7 %all-to-all-start = ((f32[8,256,256]{2,1,0:T(8,128)}), f32[8,256,256]{2,1,0:T(8,128)S(1)}, u32[]{:S(2)}, u32[]{:S(2)}) async-start(f32[8,256,256]{2,1,0:T(8,128)} %broadcast_in_dim.9), calls=%async_computation.1 | async-start | bytes 4194304 | tf_op jit(solution)/shard_map/all_to_all | solution.py:205
  71.6 69.9 %reduce-scatter.2.cloned.1.call-start = ((), (), s32[]{:S(2)}) async-start(), calls=%async_computation.3 | async-start | bytes 278528 | tf_op jit(solution)/shard_map/reduce_scatter | solution.py:224
Sparse Core Ops, SparseCore 0:
  81.0 60.4 reduce-scatter.1

commit v5 on v4

--- a/solution.py
+++ b/solution.py
@@ -113,9 +113,8 @@
     )
 
 
-def sweep_kernel(g_ref, out_ref):
-    n = g_ref.shape[0]
-    out_ref[...] = g_ref[...]
+def sweep_in_place(a_ref):
+    n = a_ref.shape[0]
     lane = lax.broadcasted_iota(jnp.int32, (1, n), 1)
 
     def step(k, row):
@@ -126,25 +125,149 @@
         column = jnp.transpose(jnp.broadcast_to(row, (TILE, n)))
         following = jnp.minimum(k + 1, n - 1)
         next_factor = jnp.sum(jnp.where(lane == following, row, 0.0), axis=1, keepdims=True)
-        next_row = out_ref[pl.ds(following, 1), :] - next_factor * scaled
+        next_row = a_ref[pl.ds(following, 1), :] - next_factor * scaled
         for h in range(n // TILE):
             lanes = slice(h * TILE, (h + 1) * TILE)
-            out_ref[:, lanes] = out_ref[:, lanes] - column * scaled[:, lanes]
-        out_ref[pl.ds(k, 1), :] = jnp.where(is_k, -inv, row * inv)
+            a_ref[:, lanes] = a_ref[:, lanes] - column * scaled[:, lanes]
+        a_ref[pl.ds(k, 1), :] = jnp.where(is_k, -inv, row * inv)
         return next_row
 
-    lax.fori_loop(0, n, step, out_ref[0:1, :], unroll=4)
-    out_ref[...] = -out_ref[...]
-
-
-def spd_inverse(gram):
+    lax.fori_loop(0, n, step, a_ref[0:1, :], unroll=4)
+    a_ref[...] = -a_ref[...]
+
+
+def tail_kernel(n_build, n_test, part_ref, test_gram_ref, build_gram_ref, owned_ref, inv_ref,
+                rs_buf, test_buf, build_buf, product_buf, gram_buf,
+                rs_send, rs_recv, test_send, test_recv, build_send, build_recv,
+                gram_send, gram_recv):
+    b = lax.axis_index("build")
+    t = lax.axis_index("test")
+    s = lax.axis_index("stmt")
+    n_rs = n_build * n_test
+    rs_rows = part_ref.shape[0] // n_rs
+    g_rows = test_gram_ref.shape[0] // n_test
+    me = b * n_test + t
+
+    def rs_copy(m, dst_slot):
+        return pltpu.make_async_remote_copy(
+            src_ref=part_ref.at[pl.ds(m * rs_rows, rs_rows)], dst_ref=rs_buf.at[dst_slot],
+            send_sem=rs_send.at[m], recv_sem=rs_recv.at[dst_slot],
+            device_id=(m // n_test, m % n_test, s), device_id_type=MESH)
+
+    def test_copy(j, dst_slot):
+        return pltpu.make_async_remote_copy(
+            src_ref=test_gram_ref.at[pl.ds(j * g_rows, g_rows)], dst_ref=test_buf.at[dst_slot],
+            send_sem=test_send.at[j], recv_sem=test_recv.at[dst_slot],
+            device_id=(b, j, s), device_id_type=MESH)
+
+    def build_copy(j, dst_slot):
+        return pltpu.make_async_remote_copy(
+            src_ref=build_gram_ref, dst_ref=build_buf.at[dst_slot],
+            send_sem=build_send.at[j], recv_sem=build_recv.at[dst_slot],
+            device_id=(j, t, s), device_id_type=MESH)
+
+    def gram_copy(j, dst_slot):
+        return pltpu.make_async_remote_copy(
+            src_ref=product_buf, dst_ref=gram_buf.at[dst_slot],
+            send_sem=gram_send.at[j], recv_sem=gram_recv.at[dst_slot],
+            device_id=(b, j, s), device_id_type=MESH)
+
+    for j in range(n_build):
+        @pl.when(j != b)
+        def _():
+            build_copy(j, b).start()
+    for j in range(n_test):
+        @pl.when(j != t)
+        def _():
+            test_copy(j, t).start()
+    for m in range(n_rs):
+        @pl.when(m != me)
+        def _():
+            rs_copy(m, me).start()
+    build_buf[pl.ds(b, 1)] = build_gram_ref[...][None]
+    test_buf[pl.ds(t, 1)] = test_gram_ref[pl.ds(pl.multiple_of(t * g_rows, g_rows), g_rows), :][None]
+    rs_buf[pl.ds(me, 1)] = part_ref[pl.ds(pl.multiple_of(me * rs_rows, rs_rows), rs_rows), :][None]
+
+    for j in range(n_build):
+        @pl.when(j != b)
+        def _():
+            build_copy(j, b).wait_send()
+            build_copy(j, j).wait_recv()
+    for j in range(n_test):
+        @pl.when(j != t)
+        def _():
+            test_copy(j, t).wait_send()
+            test_copy(j, j).wait_recv()
+
+    my_rows = pl.ds(pl.multiple_of(t * g_rows, g_rows), g_rows)
+    test_rows = test_buf[0]
+    for j in range(1, n_test):
+        test_rows = test_rows + test_buf[j]
+    build_rows = build_buf[0, my_rows, :]
+    for j in range(1, n_build):
+        build_rows = build_rows + build_buf[j, my_rows, :]
+    product_buf[...] = test_rows * build_rows
+
+    for j in range(n_test):
+        @pl.when(j != t)
+        def _():
+            gram_copy(j, t).start()
+    gram_buf[pl.ds(t, 1)] = product_buf[...][None]
+    for j in range(n_test):
+        @pl.when(j != t)
+        def _():
+            gram_copy(j, t).wait_send()
+            gram_copy(j, j).wait_recv()
+    for j in range(n_test):
+        inv_ref[j * g_rows:(j + 1) * g_rows, :] = gram_buf[j]
+
+    sweep_in_place(inv_ref)
+
+    for m in range(n_rs):
+        @pl.when(m != me)
+        def _():
+            rs_copy(m, me).wait_send()
+            rs_copy(m, m).wait_recv()
+    owned = rs_buf[0]
+    for m in range(1, n_rs):
+        owned = owned + rs_buf[m]
+    owned_ref[...] = owned
+
+
+def exchange_and_invert(partial, test_gram, build_gram):
+    n_build = lax.axis_size("build")
+    n_test = lax.axis_size("test")
+    n_rs = n_build * n_test
+    rows, rank = partial.shape
+    rs_rows = rows // n_rs
+    g_rows = rank // n_test
     vmem = pl.BlockSpec(memory_space=pltpu.VMEM)
+    f32 = jnp.float32
     return pl.pallas_call(
-        sweep_kernel,
-        out_shape=jax.ShapeDtypeStruct(gram.shape, jnp.float32),
-        in_specs=[vmem],
-        out_specs=vmem,
-    )(gram)
+        functools.partial(tail_kernel, n_build, n_test),
+        out_shape=(
+            jax.ShapeDtypeStruct((rs_rows, rank), f32),
+            jax.ShapeDtypeStruct((rank, rank), f32),
+        ),
+        in_specs=[vmem, vmem, vmem],
+        out_specs=(vmem, vmem),
+        scratch_shapes=[
+            pltpu.VMEM((n_rs, rs_rows, rank), f32),
+            pltpu.VMEM((n_test, g_rows, rank), f32),
+            pltpu.VMEM((n_build, rank, rank), f32),
+            pltpu.VMEM((g_rows, rank), f32),
+            pltpu.VMEM((n_test, g_rows, rank), f32),
+            pltpu.SemaphoreType.DMA((n_rs,)),
+            pltpu.SemaphoreType.DMA((n_rs,)),
+            pltpu.SemaphoreType.DMA((n_test,)),
+            pltpu.SemaphoreType.DMA((n_test,)),
+            pltpu.SemaphoreType.DMA((n_build,)),
+            pltpu.SemaphoreType.DMA((n_build,)),
+            pltpu.SemaphoreType.DMA((n_test,)),
+            pltpu.SemaphoreType.DMA((n_test,)),
+        ],
+        compiler_params=pltpu.CompilerParams(has_side_effects=True),
+    )(partial, test_gram, build_gram)
 
 
 def mttkrp_kernel(chunk, slot_info, test_ref, build_ref, tile_ref, out_ref, acc_ref):
@@ -200,16 +323,6 @@
     )(slot_info, test_slab, build_slab, slot_values)
 
 
-def copy_for_each(x, axis):
-    copies = jnp.broadcast_to(x, (lax.axis_size(axis), *x.shape))
-    return lax.all_to_all(copies, axis, split_axis=0, concat_axis=0, tiled=True)
-
-
-def over_copies(x, axis):
-    everything = copy_for_each(x, axis)
-    return jnp.sum(everything, axis=0)
-
-
 def shards(tile_values, tile_test, tile_stmt, tile_build, tile_count, test_factor, build_factor):
     test_slab, build_slab = gather_factors(test_factor[0], build_factor[0])
     slot_values = tile_values[0, 0, 0]
@@ -221,13 +334,9 @@
         tile_count[0, 0, 0][None],
     ]).astype(jnp.int32)
     running_sum = local_mttkrp(slot_values, slot_info, test_slab, build_slab)
-    owned_sums = lax.psum_scatter(running_sum, ("build", "test"), scatter_dimension=0, tiled=True)
     slab_test_gram = jnp.dot(test_slab.T, test_slab, preferred_element_type=jnp.float32)
     slab_build_gram = jnp.dot(build_slab.T, build_slab, preferred_element_type=jnp.float32)
-    gram_test = over_copies(slab_test_gram, "test")
-    gram_build = over_copies(slab_build_gram, "build")
-    gram = gram_test * gram_build
-    inverse = spd_inverse(gram)
+    owned_sums, inverse = exchange_and_invert(running_sum, slab_test_gram, slab_build_gram)
     solved = jnp.dot(owned_sums, inverse, precision=lax.Precision.HIGHEST, preferred_element_type=jnp.float32)
     return solved[None]
 

time: 152 us -> 119 us (0.78); the launches traced: 150 us -> 119 us
  waiting for transfers between devices: 34.2 us -> 0 us
  Pallas kernels: 78.4 us -> 110 us
  starting transfers between devices: 14.8 us -> 0 us
  between operations: 14.2 us -> 0.69 us
    pallas_call x1, Pallas kernels: 33 us -> 65 us  [exchange_and_invert(): pl.pallas_call(functools.partial(tail_kernel, n_build, n_test), out_shape...]
    all_to_all x2 -> x0, waiting for transfers between devices: 24.5 us -> none  [copy_for_each(): return lax.all_to_all(copies, axis, split_axis=0, concat_axis=0, tiled=True)]
    all_to_all x2 -> x0, starting transfers between devices: 14.8 us -> none  [copy_for_each(): return lax.all_to_all(copies, axis, split_axis=0, concat_axis=0, tiled=True)]
    reduce_scatter x1 -> x0, waiting for transfers between devices: 9.67 us -> none  [shards(): lax.psum_scatter(running_sum, ('build', 'test'), scatter_dimension=0, til...]
    broadcast_in_dim x2 -> x0, local copies, waits for them, and re-layouts: 2.34 us -> none  [copy_for_each(): copies = jnp.broadcast_to(x, (lax.axis_size(axis), *x.shape))]
  transfers between devices with their start and end apart: 3 -> 0, of which waited for: 3 -> 0; matrix products, arithmetic and copies ran while one was open for 2% -> 0% of each run, Pallas kernels for 27% -> 0%
where the time goes in v5:
time: 119 us
  Pallas kernels  110 us (92%)
  matrix products  3.77 us (3%)
  local copies, waits for them, and re-layouts  1.99 us (2%)
  other arithmetic  1.95 us (2%)
    pallas_call x1, Pallas kernels, exchange_and_invert(): pl.pallas_call(functools.partial(tail_kernel, n_build, n_test), out_shape...  65 us
    pallas_call x1, Pallas kernels, gather_factors(): pl.pallas_call(functools.partial(gather_kernel, n_build, n_test, n_stmt),...  38.4 us
    pallas_call x1, Pallas kernels, local_mttkrp(): pl.pallas_call(functools.partial(mttkrp_kernel, CHUNK), out_shape=jax.Sha...  7.03 us

profile of v5, /device:TPU:1, one launch (start us, length us, event | category | flops | bytes accessed | tf_op | source)
XLA Modules:
  0.0 118.9 jit_solution(4008627421281496585)
XLA Ops:
  0.0 38.4 %shard_map.73 = (bf16[32,16,256]{2,1,0:T(8,128)(2,1)}, bf16[128,6,256]{2,1,0:T(8,128)(2,1)}) custom-call(bf16[16,256]{1,0:T(8,128)(2,1)} %bitcast.24, bf16[6,256]{1,0:T(8,128)(2,1)} %bitcast.25), custom_call_target="tpu_custom_call" | custom-call | tf_op jit(solution)/shard_map/pallas_call | solution.py:92
  38.4 0.0 copy-start
  38.4 0.0 copy-start.1
  38.4 2.0 %reshape.16.build_ref = bf16[768,256]{1,0:T(8,128)(2,1)} reshape(bf16[128,6,256]{2,1,0:T(8,128)(2,1)} %get-tuple-element.10) | data formatting | bytes 786432 | tf_op jit(solution)/shard_map/reshape | solution.py:112
  40.4 0.7 clamp_bitcast_fusion
  41.7 0.7 clamp_bitcast_fusion.2
  42.4 0.6 pad_add_fusion.slot_info
  43.0 7.0 %shard_map.74.part_ref = f32[256,256]{1,0:T(8,128)} custom-call(s32[7]{0:T(128)} %pad_add_fusion.slot_info, bf16[512,256]{1,0:T(8,128)(2,1)} %bitcast.23, bf16[768,256]{1,0:T(8,128)(2,1)} %reshape.16.build_ref, bf16[2,128,128,128]{3,2,1,0:T(8,128)(2,1)} %bitcast.22), custom_call_target="tpu_custom_call" | custom-call | tf_op jit(solution)/shard_map/pallas_call | solution.py:319
  50.0 0.0 copy-done
  50.0 1.0 convolution_bitcast_fusion.build_gram_ref
  51.0 0.0 copy-done.1
  51.0 1.0 convolution_bitcast_fusion.1.test_gram_ref
  52.0 65.0 %shard_map.75 = (f32[16,256]{1,0:T(8,128)}, f32[256,256]{1,0:T(8,128)}) custom-call(f32[256,256]{1,0:T(8,128)} %shard_map.74.part_ref, f32[256,256]{1,0:T(8,128)} %convolution_bitcast_fusion.1.test_gram_ref, f32[256,256]{1,0:T(8,128)} %convolution_bitcast_fusion.build_gram_ref), custom_call_target="tpu_custom_call" | custom-call | tf_op jit(solution)/shard_map/pallas_call | solution.py:246
  117.1 1.8 %convolution_bitcast_fusion.2 = f32[1,16,256]{2,1,0:T(8,128)} fusion(f32[16,256]{1,0:T(8,128)} %get-tuple-element.11, f32[256,256]{1,0:T(8,128)} %get-tuple-element.12), kind=kOutput, calls=%fused_computation.2 | convolution fusion | flops 12582912 | bytes 294912 | tf_op jit(solution)/shard_map/dot_general | solution.py:340
Async XLA Ops:
  38.4 11.6 %copy-start = (bf16[128,6,256]{2,1,0:T(8,128)(2,1)S(1)}, bf16[128,6,256]{2,1,0:T(8,128)(2,1)}, u32[]{:S(2)}) copy-start(bf16[128,6,256]{2,1,0:T(8,128)(2,1)} %get-tuple-element.10) | copy-start | bytes 1179652
  38.4 12.6 %copy-start.1 = (bf16[32,16,256]{2,1,0:T(8,128)(2,1)S(1)}, bf16[32,16,256]{2,1,0:T(8,128)(2,1)}, u32[]{:S(2)}) copy-start(bf16[32,16,256]{2,1,0:T(8,128)(2,1)} %get-tuple-element.9) | copy-start | bytes 786436

commit v6 on v5

--- a/solution.py
+++ b/solution.py
@@ -44,6 +44,24 @@
             src_ref=build_in, dst_ref=build_scr.at[q], send_sem=build_send.at[q],
             recv_sem=build_recv.at[q], device_id=(b, q // n_stmt, q % n_stmt),
             device_id_type=MESH)
+
+    barrier = pltpu.get_barrier_semaphore()
+
+    def greet_test(p, carry):
+        @pl.when(p != my_p)
+        def _():
+            pl.semaphore_signal(barrier, 1, device_id=(p // n_stmt, t, p % n_stmt), device_id_type=MESH)
+        return carry
+
+    def greet_build(q, carry):
+        @pl.when(q != my_q)
+        def _():
+            pl.semaphore_signal(barrier, 1, device_id=(b, q // n_stmt, q % n_stmt), device_id_type=MESH)
+        return carry
+
+    lax.fori_loop(0, n_build * n_stmt, greet_test, 0)
+    lax.fori_loop(0, n_test * n_stmt, greet_build, 0)
+    pl.semaphore_wait(barrier, n_build * n_stmt + n_test * n_stmt - 2)
 
     def start_test(p, carry):
         @pl.when(p != my_p)
@@ -105,7 +123,7 @@
             pltpu.SemaphoreType.DMA((n_q,)),
             pltpu.SemaphoreType.DMA((n_q,)),
         ],
-        compiler_params=pltpu.CompilerParams(has_side_effects=True),
+        compiler_params=pltpu.CompilerParams(has_side_effects=True, collective_id=0),
     )(test_rows, build_rows)
     return (
         test_pieces.reshape(-1, test_rows.shape[-1]),
@@ -171,6 +189,13 @@
             src_ref=product_buf, dst_ref=gram_buf.at[dst_slot],
             send_sem=gram_send.at[j], recv_sem=gram_recv.at[dst_slot],
             device_id=(b, j, s), device_id_type=MESH)
+
+    barrier = pltpu.get_barrier_semaphore()
+    for m in range(n_rs):
+        @pl.when(m != me)
+        def _():
+            pl.semaphore_signal(barrier, 1, device_id=(m // n_test, m % n_test, s), device_id_type=MESH)
+    pl.semaphore_wait(barrier, n_rs - 1)
 
     for j in range(n_build):
         @pl.when(j != b)
@@ -266,7 +291,7 @@
             pltpu.SemaphoreType.DMA((n_test,)),
             pltpu.SemaphoreType.DMA((n_test,)),
         ],
-        compiler_params=pltpu.CompilerParams(has_side_effects=True),
+        compiler_params=pltpu.CompilerParams(has_side_effects=True, collective_id=1),
     )(partial, test_gram, build_gram)
 
 

time: 119 us -> 109 us (0.916)
  Pallas kernels: 110 us -> 100 us
    pallas_call x1, Pallas kernels: 65 us -> 58.4 us  [exchange_and_invert(): pl.pallas_call(functools.partial(tail_kernel, n_build, n_test), out_shape...]
    pallas_call x1, Pallas kernels: 38.4 us -> 34.5 us  [gather_factors(): pl.pallas_call(functools.partial(gather_kernel, n_build, n_test, n_stmt),...]
where the time goes in v6:
time: 109 us; the launch traced here: 108 us
  Pallas kernels  100 us (92%)
  matrix products  3.77 us (3%)
  local copies, waits for them, and re-layouts  1.99 us (2%)
  other arithmetic  1.95 us (2%)
    pallas_call x1, Pallas kernels, exchange_and_invert(): pl.pallas_call(functools.partial(tail_kernel, n_build, n_test), out_shape...  58.4 us
    pallas_call x1, Pallas kernels, gather_factors(): pl.pallas_call(functools.partial(gather_kernel, n_build, n_test, n_stmt),...  34.5 us
    pallas_call x1, Pallas kernels, local_mttkrp(): pl.pallas_call(functools.partial(mttkrp_kernel, CHUNK), out_shape=jax.Sha...  7.03 us

profile of v6, /device:TPU:1, one launch (start us, length us, event | category | flops | bytes accessed | tf_op | source)
XLA Modules:
  0.0 108.4 jit_solution(16475557163471225744)
XLA Ops:
  0.0 34.5 %shard_map.73 = (bf16[32,16,256]{2,1,0:T(8,128)(2,1)}, bf16[128,6,256]{2,1,0:T(8,128)(2,1)}) custom-call(bf16[16,256]{1,0:T(8,128)(2,1)} %bitcast.24, bf16[6,256]{1,0:T(8,128)(2,1)} %bitcast.25), custom_call_target="tpu_custom_call" | custom-call | tf_op jit(solution)/shard_map/pallas_call | solution.py:110
  34.5 0.0 copy-start
  34.5 0.0 copy-start.1
  34.5 2.0 %reshape.16.build_ref = bf16[768,256]{1,0:T(8,128)(2,1)} reshape(bf16[128,6,256]{2,1,0:T(8,128)(2,1)} %get-tuple-element.10) | data formatting | bytes 786432 | tf_op jit(solution)/shard_map/reshape | solution.py:130
  36.5 0.7 clamp_bitcast_fusion
  37.9 0.7 clamp_bitcast_fusion.2
  38.5 0.6 pad_add_fusion.slot_info
  39.1 7.0 %shard_map.74.part_ref = f32[256,256]{1,0:T(8,128)} custom-call(s32[7]{0:T(128)} %pad_add_fusion.slot_info, bf16[512,256]{1,0:T(8,128)(2,1)} %bitcast.23, bf16[768,256]{1,0:T(8,128)(2,1)} %reshape.16.build_ref, bf16[2,128,128,128]{3,2,1,0:T(8,128)(2,1)} %bitcast.22), custom_call_target="tpu_custom_call" | custom-call | tf_op jit(solution)/shard_map/pallas_call | solution.py:344
  46.2 0.0 copy-done
  46.2 1.0 convolution_bitcast_fusion.build_gram_ref
  47.2 0.0 copy-done.1
  47.2 1.0 convolution_bitcast_fusion.1.test_gram_ref
  48.1 58.4 %shard_map.75 = (f32[16,256]{1,0:T(8,128)}, f32[256,256]{1,0:T(8,128)}) custom-call(f32[256,256]{1,0:T(8,128)} %shard_map.74.part_ref, f32[256,256]{1,0:T(8,128)} %convolution_bitcast_fusion.1.test_gram_ref, f32[256,256]{1,0:T(8,128)} %convolution_bitcast_fusion.build_gram_ref), custom_call_target="tpu_custom_call" | custom-call | tf_op jit(solution)/shard_map/pallas_call | solution.py:271
  106.6 1.8 %convolution_bitcast_fusion.2 = f32[1,16,256]{2,1,0:T(8,128)} fusion(f32[16,256]{1,0:T(8,128)} %get-tuple-element.11, f32[256,256]{1,0:T(8,128)} %get-tuple-element.12), kind=kOutput, calls=%fused_computation.2 | convolution fusion | flops 12582912 | bytes 294912 | tf_op jit(solution)/shard_map/dot_general | solution.py:365
Async XLA Ops:
  34.5 11.6 %copy-start = (bf16[128,6,256]{2,1,0:T(8,128)(2,1)S(1)}, bf16[128,6,256]{2,1,0:T(8,128)(2,1)}, u32[]{:S(2)}) copy-start(bf16[128,6,256]{2,1,0:T(8,128)(2,1)} %get-tuple-element.10) | copy-start | bytes 1179652
  34.5 12.6 %copy-start.1 = (bf16[32,16,256]{2,1,0:T(8,128)(2,1)S(1)}, bf16[32,16,256]{2,1,0:T(8,128)(2,1)}, u32[]{:S(2)}) copy-start(bf16[32,16,256]{2,1,0:T(8,128)(2,1)} %get-tuple-element.9) | copy-start | bytes 786436

commit v7 on v5

--- a/solution.py
+++ b/solution.py
@@ -14,70 +14,84 @@
 
 
 def gather_kernel(n_build, n_test, n_stmt, test_in, build_in, test_out, build_out,
-                  test_scr, build_scr, test_send, test_recv, build_send, build_recv):
+                  test_scr, build_scr, local_sem, t1_send, t1_recv, b1_send, b1_recv,
+                  t2_send, t2_recv, b2_send, b2_recv):
     b = lax.axis_index("build")
     t = lax.axis_index("test")
     s = lax.axis_index("stmt")
-    my_p = b * n_stmt + s
-    my_q = t * n_stmt + s
-
-    def test_out_copy(p):
-        return pltpu.make_async_remote_copy(
-            src_ref=test_in, dst_ref=test_scr.at[my_p], send_sem=test_send.at[p],
-            recv_sem=test_recv.at[my_p], device_id=(p // n_stmt, t, p % n_stmt),
-            device_id_type=MESH)
-
-    def test_in_copy(p):
-        return pltpu.make_async_remote_copy(
-            src_ref=test_in, dst_ref=test_scr.at[p], send_sem=test_send.at[p],
-            recv_sem=test_recv.at[p], device_id=(p // n_stmt, t, p % n_stmt),
-            device_id_type=MESH)
-
-    def build_out_copy(q):
-        return pltpu.make_async_remote_copy(
-            src_ref=build_in, dst_ref=build_scr.at[my_q], send_sem=build_send.at[q],
-            recv_sem=build_recv.at[my_q], device_id=(b, q // n_stmt, q % n_stmt),
-            device_id_type=MESH)
-
-    def build_in_copy(q):
-        return pltpu.make_async_remote_copy(
-            src_ref=build_in, dst_ref=build_scr.at[q], send_sem=build_send.at[q],
-            recv_sem=build_recv.at[q], device_id=(b, q // n_stmt, q % n_stmt),
-            device_id_type=MESH)
-
-    def start_test(p, carry):
-        @pl.when(p != my_p)
-        def _():
-            test_out_copy(p).start()
-        return carry
-
-    def start_build(q, carry):
-        @pl.when(q != my_q)
-        def _():
-            build_out_copy(q).start()
-        return carry
-
-    lax.fori_loop(0, n_build * n_stmt, start_test, 0)
-    lax.fori_loop(0, n_test * n_stmt, start_build, 0)
-    test_scr[pl.ds(my_p, 1)] = test_in[...][None]
-    build_scr[pl.ds(my_q, 1)] = build_in[...][None]
-
-    def wait_test(p, carry):
-        @pl.when(p != my_p)
-        def _():
-            test_out_copy(p).wait_send()
-            test_in_copy(p).wait_recv()
-        return carry
-
-    def wait_build(q, carry):
-        @pl.when(q != my_q)
-        def _():
-            build_out_copy(q).wait_send()
-            build_in_copy(q).wait_recv()
-        return carry
-
-    lax.fori_loop(0, n_build * n_stmt, wait_test, 0)
-    lax.fori_loop(0, n_test * n_stmt, wait_build, 0)
+
+    barrier = pltpu.get_barrier_semaphore()
+    for j in range(n_stmt):
+        @pl.when(j != s)
+        def _():
+            pl.semaphore_signal(barrier, 1, device_id=(b, t, j), device_id_type=MESH)
+    for j in range(n_build):
+        @pl.when(j != b)
+        def _():
+            pl.semaphore_signal(barrier, 1, device_id=(j, t, s), device_id_type=MESH)
+    for j in range(n_test):
+        @pl.when(j != t)
+        def _():
+            pl.semaphore_signal(barrier, 1, device_id=(b, j, s), device_id_type=MESH)
+    pl.semaphore_wait(barrier, n_stmt + n_build + n_test - 3)
+
+    def t1(j, slot):
+        return pltpu.make_async_remote_copy(
+            src_ref=test_in, dst_ref=test_scr.at[b, slot], send_sem=t1_send.at[j],
+            recv_sem=t1_recv.at[slot], device_id=(b, t, j), device_id_type=MESH)
+
+    def b1(j, slot):
+        return pltpu.make_async_remote_copy(
+            src_ref=build_in, dst_ref=build_scr.at[t, slot], send_sem=b1_send.at[j],
+            recv_sem=b1_recv.at[slot], device_id=(b, t, j), device_id_type=MESH)
+
+    def t2(j, slot):
+        return pltpu.make_async_remote_copy(
+            src_ref=test_scr.at[b], dst_ref=test_scr.at[slot], send_sem=t2_send.at[j],
+            recv_sem=t2_recv.at[slot], device_id=(j, t, s), device_id_type=MESH)
+
+    def b2(j, slot):
+        return pltpu.make_async_remote_copy(
+            src_ref=build_scr.at[t], dst_ref=build_scr.at[slot], send_sem=b2_send.at[j],
+            recv_sem=b2_recv.at[slot], device_id=(b, j, s), device_id_type=MESH)
+
+    for j in range(n_stmt):
+        @pl.when(j != s)
+        def _():
+            t1(j, s).start()
+            b1(j, s).start()
+    own_test = pltpu.make_async_copy(test_in, test_scr.at[b, s], local_sem.at[0])
+    own_build = pltpu.make_async_copy(build_in, build_scr.at[t, s], local_sem.at[1])
+    own_test.start()
+    own_build.start()
+    own_test.wait()
+    own_build.wait()
+    for j in range(n_stmt):
+        @pl.when(j != s)
+        def _():
+            t1(j, s).wait_send()
+            b1(j, s).wait_send()
+            t1(j, j).wait_recv()
+            b1(j, j).wait_recv()
+
+    for j in range(n_build):
+        @pl.when(j != b)
+        def _():
+            t2(j, b).start()
+    for j in range(n_test):
+        @pl.when(j != t)
+        def _():
+            b2(j, t).start()
+    for j in range(n_build):
+        @pl.when(j != b)
+        def _():
+            t2(j, b).wait_send()
+            t2(j, j).wait_recv()
+    for j in range(n_test):
+        @pl.when(j != t)
+        def _():
+            b2(j, t).wait_send()
+            b2(j, j).wait_recv()
     test_out[...] = test_scr[...]
     build_out[...] = build_scr[...]
 
@@ -86,26 +100,26 @@
     n_build = lax.axis_size("build")
     n_test = lax.axis_size("test")
     n_stmt = lax.axis_size("stmt")
-    n_p = n_build * n_stmt
-    n_q = n_test * n_stmt
     vmem = pl.BlockSpec(memory_space=pltpu.VMEM)
+    test_shape = (n_build, n_stmt, *test_rows.shape)
+    build_shape = (n_test, n_stmt, *build_rows.shape)
+    dma = pltpu.SemaphoreType.DMA
     test_pieces, build_pieces = pl.pallas_call(
         functools.partial(gather_kernel, n_build, n_test, n_stmt),
         out_shape=(
-            jax.ShapeDtypeStruct((n_p, *test_rows.shape), test_rows.dtype),
-            jax.ShapeDtypeStruct((n_q, *build_rows.shape), build_rows.dtype),
+            jax.ShapeDtypeStruct(test_shape, test_rows.dtype),
+            jax.ShapeDtypeStruct(build_shape, build_rows.dtype),
         ),
         in_specs=[vmem, vmem],
         out_specs=(vmem, vmem),
         scratch_shapes=[
-            pltpu.VMEM((n_p, *test_rows.shape), test_rows.dtype),
-            pltpu.VMEM((n_q, *build_rows.shape), build_rows.dtype),
-            pltpu.SemaphoreType.DMA((n_p,)),
-            pltpu.SemaphoreType.DMA((n_p,)),
-            pltpu.SemaphoreType.DMA((n_q,)),
-            pltpu.SemaphoreType.DMA((n_q,)),
+            pltpu.VMEM(test_shape, test_rows.dtype),
+            pltpu.VMEM(build_shape, build_rows.dtype),
+            dma((2,)),
+            dma((n_stmt,)), dma((n_stmt,)), dma((n_stmt,)), dma((n_stmt,)),
+            dma((n_build,)), dma((n_build,)), dma((n_test,)), dma((n_test,)),
         ],
-        compiler_params=pltpu.CompilerParams(has_side_effects=True),
+        compiler_params=pltpu.CompilerParams(has_side_effects=True, collective_id=0),
     )(test_rows, build_rows)
     return (
         test_pieces.reshape(-1, test_rows.shape[-1]),
@@ -171,6 +185,13 @@
             src_ref=product_buf, dst_ref=gram_buf.at[dst_slot],
             send_sem=gram_send.at[j], recv_sem=gram_recv.at[dst_slot],
             device_id=(b, j, s), device_id_type=MESH)
+
+    barrier = pltpu.get_barrier_semaphore()
+    for m in range(n_rs):
+        @pl.when(m != me)
+        def _():
+            pl.semaphore_signal(barrier, 1, device_id=(m // n_test, m % n_test, s), device_id_type=MESH)
+    pl.semaphore_wait(barrier, n_rs - 1)
 
     for j in range(n_build):
         @pl.when(j != b)
@@ -266,7 +287,7 @@
             pltpu.SemaphoreType.DMA((n_test,)),
             pltpu.SemaphoreType.DMA((n_test,)),
         ],
-        compiler_params=pltpu.CompilerParams(has_side_effects=True),
+        compiler_params=pltpu.CompilerParams(has_side_effects=True, collective_id=1),
     )(partial, test_gram, build_gram)
 
 

time: 119 us -> 94.5 us (0.79)
  Pallas kernels: 110 us -> 85.7 us
    pallas_call x1, Pallas kernels: 65 us -> 50 us  [exchange_and_invert(): pl.pallas_call(functools.partial(tail_kernel, n_build, n_test), out_shape...]
    pallas_call x1, Pallas kernels: 38.4 us -> 25.3 us  [gather_factors(): pl.pallas_call(functools.partial(gather_kernel, n_build, n_test, n_stmt),...]
    pallas_call x1, Pallas kernels: 7.03 us -> 10.4 us  [local_mttkrp(): pl.pallas_call(functools.partial(mttkrp_kernel, CHUNK), out_shape=jax.Sha...]
where the time goes in v7:
time: 94.5 us; the launch traced here: 94.1 us
  Pallas kernels  85.7 us (91%)
  matrix products  3.77 us (4%)
  local copies, waits for them, and re-layouts  1.99 us (2%)
  other arithmetic  1.95 us (2%)
    pallas_call x1, Pallas kernels, exchange_and_invert(): pl.pallas_call(functools.partial(tail_kernel, n_build, n_test), out_shape...  50 us
    pallas_call x1, Pallas kernels, gather_factors(): pl.pallas_call(functools.partial(gather_kernel, n_build, n_test, n_stmt),...  25.3 us
    pallas_call x1, Pallas kernels, local_mttkrp(): pl.pallas_call(functools.partial(mttkrp_kernel, CHUNK), out_shape=jax.Sha...  10.4 us
    reshape x1, local copies, waits for them, and re-layouts, gather_factors(): build_pieces.reshape(-1, build_rows.shape[-1])  1.99 us

profile of v7, /device:TPU:1, one launch (start us, length us, event | category | flops | bytes accessed | tf_op | source)
XLA Modules:
  0.0 94.1 jit_solution(13727732923418268852)
XLA Ops:
  0.0 25.3 %shard_map.73 = (bf16[2,16,16,256]{3,2,1,0:T(8,128)(2,1)}, bf16[8,16,6,256]{3,2,1,0:T(8,128)(2,1)}) custom-call(bf16[16,256]{1,0:T(8,128)(2,1)} %bitcast.28, bf16[6,256]{1,0:T(8,128)(2,1)} %bitcast.29), custom_call_target="tpu_custom_call" | custom-call | tf_op jit(solution)/shard_map/pallas_call | solution.py:107
  25.3 0.0 copy-start
  25.3 0.0 copy-start.1
  25.3 2.0 %reshape.16.build_ref = bf16[768,256]{1,0:T(8,128)(2,1)} reshape(bf16[8,16,6,256]{3,2,1,0:T(8,128)(2,1)} %get-tuple-element.10) | data formatting | bytes 786432 | tf_op jit(solution)/shard_map/reshape | solution.py:126
  27.3 0.7 clamp_bitcast_fusion
  28.7 0.7 clamp_bitcast_fusion.2
  29.3 0.6 pad_add_fusion.slot_info
  29.9 10.4 %shard_map.74.part_ref = f32[256,256]{1,0:T(8,128)} custom-call(s32[7]{0:T(128)} %pad_add_fusion.slot_info, bf16[512,256]{1,0:T(8,128)(2,1)} %bitcast.27, bf16[768,256]{1,0:T(8,128)(2,1)} %reshape.16.build_ref, bf16[2,128,128,128]{3,2,1,0:T(8,128)(2,1)} %bitcast.26), custom_call_target="tpu_custom_call" | custom-call | tf_op jit(solution)/shard_map/pallas_call | solution.py:340
  40.3 0.0 copy-done
  40.3 1.0 %convolution_bitcast_fusion.build_gram_ref = f32[256,256]{1,0:T(8,128)} fusion(bf16[8,16,6,256]{3,2,1,0:T(8,128)(2,1)S(1)} %copy-done), kind=kOutput, calls=%fused_computation | convolution fusion | flops 100663296 | bytes 655360 | tf_op jit(solution)/shard_map/dot_general | solution.py:359
  41.3 0.0 copy-done.1
  41.3 1.0 %convolution_bitcast_fusion.1.test_gram_ref = f32[256,256]{1,0:T(8,128)} fusion(bf16[2,16,16,256]{3,2,1,0:T(8,128)(2,1)S(1)} %copy-done.1), kind=kOutput, calls=%fused_computation.1 | convolution fusion | flops 67108864 | bytes 524288 | tf_op jit(solution)/shard_map/dot_general | solution.py:358
  42.3 50.0 %shard_map.75 = (f32[16,256]{1,0:T(8,128)}, f32[256,256]{1,0:T(8,128)}) custom-call(f32[256,256]{1,0:T(8,128)} %shard_map.74.part_ref, f32[256,256]{1,0:T(8,128)} %convolution_bitcast_fusion.1.test_gram_ref, f32[256,256]{1,0:T(8,128)} %convolution_bitcast_fusion.build_gram_ref), custom_call_target="tpu_custom_call" | custom-call | tf_op jit(solution)/shard_map/pallas_call | solution.py:267
  92.3 1.8 %convolution_bitcast_fusion.2 = f32[1,16,256]{2,1,0:T(8,128)} fusion(f32[16,256]{1,0:T(8,128)} %get-tuple-element.11, f32[256,256]{1,0:T(8,128)} %get-tuple-element.12), kind=kOutput, calls=%fused_computation.2 | convolution fusion | flops 12582912 | bytes 294912 | tf_op jit(solution)/shard_map/dot_general | solution.py:361
Async XLA Ops:
  25.3 15.0 %copy-start = (bf16[8,16,6,256]{3,2,1,0:T(8,128)(2,1)S(1)}, bf16[8,16,6,256]{3,2,1,0:T(8,128)(2,1)}, u32[]{:S(2)}) copy-start(bf16[8,16,6,256]{3,2,1,0:T(8,128)(2,1)} %get-tuple-element.10) | copy-start | bytes 1179652
  25.3 16.0 %copy-start.1 = (bf16[2,16,16,256]{3,2,1,0:T(8,128)(2,1)S(1)}, bf16[2,16,16,256]{3,2,1,0:T(8,128)(2,1)}, u32[]{:S(2)}) copy-start(bf16[2,16,16,256]{3,2,1,0:T(8,128)(2,1)} %get-tuple-element.9) | copy-start | bytes 786436

commit v8 on v7

--- a/solution.py
+++ b/solution.py
@@ -176,7 +176,7 @@
 
     def build_copy(j, dst_slot):
         return pltpu.make_async_remote_copy(
-            src_ref=build_gram_ref, dst_ref=build_buf.at[dst_slot],
+            src_ref=build_gram_ref.at[pl.ds(t * g_rows, g_rows)], dst_ref=build_buf.at[dst_slot],
             send_sem=build_send.at[j], recv_sem=build_recv.at[dst_slot],
             device_id=(j, t, s), device_id_type=MESH)
 
@@ -201,13 +201,8 @@
         @pl.when(j != t)
         def _():
             test_copy(j, t).start()
-    for m in range(n_rs):
-        @pl.when(m != me)
-        def _():
-            rs_copy(m, me).start()
-    build_buf[pl.ds(b, 1)] = build_gram_ref[...][None]
+    build_buf[pl.ds(b, 1)] = build_gram_ref[pl.ds(pl.multiple_of(t * g_rows, g_rows), g_rows), :][None]
     test_buf[pl.ds(t, 1)] = test_gram_ref[pl.ds(pl.multiple_of(t * g_rows, g_rows), g_rows), :][None]
-    rs_buf[pl.ds(me, 1)] = part_ref[pl.ds(pl.multiple_of(me * rs_rows, rs_rows), rs_rows), :][None]
 
     for j in range(n_build):
         @pl.when(j != b)
@@ -220,13 +215,12 @@
             test_copy(j, t).wait_send()
             test_copy(j, j).wait_recv()
 
-    my_rows = pl.ds(pl.multiple_of(t * g_rows, g_rows), g_rows)
     test_rows = test_buf[0]
     for j in range(1, n_test):
         test_rows = test_rows + test_buf[j]
-    build_rows = build_buf[0, my_rows, :]
+    build_rows = build_buf[0]
     for j in range(1, n_build):
-        build_rows = build_rows + build_buf[j, my_rows, :]
+        build_rows = build_rows + build_buf[j]
     product_buf[...] = test_rows * build_rows
 
     for j in range(n_test):
@@ -241,6 +235,12 @@
             gram_copy(j, j).wait_recv()
     for j in range(n_test):
         inv_ref[j * g_rows:(j + 1) * g_rows, :] = gram_buf[j]
+
+    for m in range(n_rs):
+        @pl.when(m != me)
+        def _():
+            rs_copy(m, me).start()
+    rs_buf[pl.ds(me, 1)] = part_ref[pl.ds(pl.multiple_of(me * rs_rows, rs_rows), rs_rows), :][None]
 
     sweep_in_place(inv_ref)
 
@@ -275,7 +275,7 @@
         scratch_shapes=[
             pltpu.VMEM((n_rs, rs_rows, rank), f32),
             pltpu.VMEM((n_test, g_rows, rank), f32),
-            pltpu.VMEM((n_build, rank, rank), f32),
+            pltpu.VMEM((n_build, g_rows, rank), f32),
             pltpu.VMEM((g_rows, rank), f32),
             pltpu.VMEM((n_test, g_rows, rank), f32),
             pltpu.SemaphoreType.DMA((n_rs,)),

time: 94.5 us -> 90.4 us (0.957)
  Pallas kernels: 85.7 us -> 81.6 us
    pallas_call x1, Pallas kernels: 50 us -> 47.3 us  [exchange_and_invert(): pl.pallas_call(functools.partial(tail_kernel, n_build, n_test), out_shape...]
    pallas_call x1, Pallas kernels: 10.4 us -> 8.93 us  [local_mttkrp(): pl.pallas_call(functools.partial(mttkrp_kernel, CHUNK), out_shape=jax.Sha...]
where the time goes in v8:
time: 90.4 us; the launch traced here: 90 us
  Pallas kernels  81.6 us (90%)
  matrix products  3.77 us (4%)
  local copies, waits for them, and re-layouts  1.99 us (2%)
  other arithmetic  1.95 us (2%)
    pallas_call x1, Pallas kernels, exchange_and_invert(): pl.pallas_call(functools.partial(tail_kernel, n_build, n_test), out_shape...  47.3 us
    pallas_call x1, Pallas kernels, gather_factors(): pl.pallas_call(functools.partial(gather_kernel, n_build, n_test, n_stmt),...  25.3 us
    pallas_call x1, Pallas kernels, local_mttkrp(): pl.pallas_call(functools.partial(mttkrp_kernel, CHUNK), out_shape=jax.Sha...  8.93 us
    reshape x1, local copies, waits for them, and re-layouts, gather_factors(): build_pieces.reshape(-1, build_rows.shape[-1])  1.99 us

profile of v8, /device:TPU:1, one launch (start us, length us, event | category | flops | bytes accessed | tf_op | source)
XLA Modules:
  0.0 90.0 jit_solution(1602665610035420446)
XLA Ops:
  0.0 25.3 %shard_map.73 = (bf16[2,16,16,256]{3,2,1,0:T(8,128)(2,1)}, bf16[8,16,6,256]{3,2,1,0:T(8,128)(2,1)}) custom-call(bf16[16,256]{1,0:T(8,128)(2,1)} %bitcast.28, bf16[6,256]{1,0:T(8,128)(2,1)} %bitcast.29), custom_call_target="tpu_custom_call" | custom-call | tf_op jit(solution)/shard_map/pallas_call | solution.py:107
  25.3 0.0 copy-start
  25.3 0.0 copy-start.1
  25.3 2.0 %reshape.16.build_ref = bf16[768,256]{1,0:T(8,128)(2,1)} reshape(bf16[8,16,6,256]{3,2,1,0:T(8,128)(2,1)} %get-tuple-element.10) | data formatting | bytes 786432 | tf_op jit(solution)/shard_map/reshape | solution.py:126
  27.3 0.7 clamp_bitcast_fusion
  28.7 0.7 clamp_bitcast_fusion.2
  29.3 0.6 pad_add_fusion.slot_info
  29.9 8.9 %shard_map.74.part_ref = f32[256,256]{1,0:T(8,128)} custom-call(s32[7]{0:T(128)} %pad_add_fusion.slot_info, bf16[512,256]{1,0:T(8,128)(2,1)} %bitcast.27, bf16[768,256]{1,0:T(8,128)(2,1)} %reshape.16.build_ref, bf16[2,128,128,128]{3,2,1,0:T(8,128)(2,1)} %bitcast.26), custom_call_target="tpu_custom_call" | custom-call | tf_op jit(solution)/shard_map/pallas_call | solution.py:340
  38.9 0.0 copy-done
  38.9 1.0 %convolution_bitcast_fusion.build_gram_ref = f32[256,256]{1,0:T(8,128)} fusion(bf16[8,16,6,256]{3,2,1,0:T(8,128)(2,1)S(1)} %copy-done), kind=kOutput, calls=%fused_computation | convolution fusion | flops 100663296 | bytes 655360 | tf_op jit(solution)/shard_map/dot_general | solution.py:359
  39.9 0.0 copy-done.1
  39.9 1.0 %convolution_bitcast_fusion.1.test_gram_ref = f32[256,256]{1,0:T(8,128)} fusion(bf16[2,16,16,256]{3,2,1,0:T(8,128)(2,1)S(1)} %copy-done.1), kind=kOutput, calls=%fused_computation.1 | convolution fusion | flops 67108864 | bytes 524288 | tf_op jit(solution)/shard_map/dot_general | solution.py:358
  40.8 47.3 %shard_map.75 = (f32[16,256]{1,0:T(8,128)}, f32[256,256]{1,0:T(8,128)}) custom-call(f32[256,256]{1,0:T(8,128)} %shard_map.74.part_ref, f32[256,256]{1,0:T(8,128)} %convolution_bitcast_fusion.1.test_gram_ref, f32[256,256]{1,0:T(8,128)} %convolution_bitcast_fusion.build_gram_ref), custom_call_target="tpu_custom_call" | custom-call | tf_op jit(solution)/shard_map/pallas_call | solution.py:267
  88.2 1.8 %convolution_bitcast_fusion.2 = f32[1,16,256]{2,1,0:T(8,128)} fusion(f32[16,256]{1,0:T(8,128)} %get-tuple-element.11, f32[256,256]{1,0:T(8,128)} %get-tuple-element.12), kind=kOutput, calls=%fused_computation.2 | convolution fusion | flops 12582912 | bytes 294912 | tf_op jit(solution)/shard_map/dot_general | solution.py:361
Async XLA Ops:
  25.3 13.5 %copy-start = (bf16[8,16,6,256]{3,2,1,0:T(8,128)(2,1)S(1)}, bf16[8,16,6,256]{3,2,1,0:T(8,128)(2,1)}, u32[]{:S(2)}) copy-start(bf16[8,16,6,256]{3,2,1,0:T(8,128)(2,1)} %get-tuple-element.10) | copy-start | bytes 1179652
  25.3 14.5 %copy-start.1 = (bf16[2,16,16,256]{3,2,1,0:T(8,128)(2,1)S(1)}, bf16[2,16,16,256]{3,2,1,0:T(8,128)(2,1)}, u32[]{:S(2)}) copy-start(bf16[2,16,16,256]{3,2,1,0:T(8,128)(2,1)} %get-tuple-element.9) | copy-start | bytes 786436

commit v9 on v8

--- a/solution.py
+++ b/solution.py
@@ -146,7 +146,7 @@
         a_ref[pl.ds(k, 1), :] = jnp.where(is_k, -inv, row * inv)
         return next_row
 
-    lax.fori_loop(0, n, step, a_ref[0:1, :], unroll=4)
+    lax.fori_loop(0, n, step, a_ref[0:1, :], unroll=8)
     a_ref[...] = -a_ref[...]
 
 

time: 90.4 us -> 88.9 us (0.983)
  the two profiles are of different devices: /device:TPU:1 before, /device:TPU:17 now
where the time goes in v9:
time: 88.9 us; the launch traced here: 88.5 us
  Pallas kernels  80.1 us (90%)
  matrix products  3.77 us (4%)
  local copies, waits for them, and re-layouts  1.99 us (2%)
  other arithmetic  1.95 us (2%)
    pallas_call x1, Pallas kernels, exchange_and_invert(): pl.pallas_call(functools.partial(tail_kernel, n_build, n_test), out_shape...  47.5 us
    pallas_call x1, Pallas kernels, gather_factors(): pl.pallas_call(functools.partial(gather_kernel, n_build, n_test, n_stmt),...  25.6 us
    pallas_call x1, Pallas kernels, local_mttkrp(): pl.pallas_call(functools.partial(mttkrp_kernel, CHUNK), out_shape=jax.Sha...  7.01 us
    reshape x1, local copies, waits for them, and re-layouts, gather_factors(): build_pieces.reshape(-1, build_rows.shape[-1])  1.99 us
    dot_general x1, matrix products, shards(): jnp.dot(owned_sums, inverse, precision=lax.Precision.HIGHEST, preferred_e...  1.8 us

profile of v9, /device:TPU:17, one launch (start us, length us, event | category | flops | bytes accessed | tf_op | source)
XLA Modules:
  0.0 88.5 jit_solution(16157575576336009700)
XLA Ops:
  0.0 25.6 %shard_map.73 = (bf16[2,16,16,256]{3,2,1,0:T(8,128)(2,1)}, bf16[8,16,6,256]{3,2,1,0:T(8,128)(2,1)}) custom-call(bf16[16,256]{1,0:T(8,128)(2,1)} %bitcast.28, bf16[6,256]{1,0:T(8,128)(2,1)} %bitcast.29), custom_call_target="tpu_custom_call" | custom-call | tf_op jit(solution)/shard_map/pallas_call | solution.py:107
  25.6 0.0 copy-start
  25.6 0.0 copy-start.1
  25.7 2.0 %reshape.16.build_ref = bf16[768,256]{1,0:T(8,128)(2,1)} reshape(bf16[8,16,6,256]{3,2,1,0:T(8,128)(2,1)} %get-tuple-element.10) | data formatting | bytes 786432 | tf_op jit(solution)/shard_map/reshape | solution.py:126
  27.6 0.7 clamp_bitcast_fusion
  29.0 0.7 clamp_bitcast_fusion.2
  29.6 0.6 pad_add_fusion.slot_info
  30.3 7.0 %shard_map.74.part_ref = f32[256,256]{1,0:T(8,128)} custom-call(s32[7]{0:T(128)} %pad_add_fusion.slot_info, bf16[512,256]{1,0:T(8,128)(2,1)} %bitcast.27, bf16[768,256]{1,0:T(8,128)(2,1)} %reshape.16.build_ref, bf16[2,128,128,128]{3,2,1,0:T(8,128)(2,1)} %bitcast.26), custom_call_target="tpu_custom_call" | custom-call | tf_op jit(solution)/shard_map/pallas_call | solution.py:340
  37.3 0.0 copy-done
  37.3 1.0 %convolution_bitcast_fusion.build_gram_ref = f32[256,256]{1,0:T(8,128)} fusion(bf16[8,16,6,256]{3,2,1,0:T(8,128)(2,1)S(1)} %copy-done), kind=kOutput, calls=%fused_computation | convolution fusion | flops 100663296 | bytes 655360 | tf_op jit(solution)/shard_map/dot_general | solution.py:359
  38.3 0.0 copy-done.1
  38.3 1.0 %convolution_bitcast_fusion.1.test_gram_ref = f32[256,256]{1,0:T(8,128)} fusion(bf16[2,16,16,256]{3,2,1,0:T(8,128)(2,1)S(1)} %copy-done.1), kind=kOutput, calls=%fused_computation.1 | convolution fusion | flops 67108864 | bytes 524288 | tf_op jit(solution)/shard_map/dot_general | solution.py:358
  39.2 47.5 %shard_map.75 = (f32[16,256]{1,0:T(8,128)}, f32[256,256]{1,0:T(8,128)}) custom-call(f32[256,256]{1,0:T(8,128)} %shard_map.74.part_ref, f32[256,256]{1,0:T(8,128)} %convolution_bitcast_fusion.1.test_gram_ref, f32[256,256]{1,0:T(8,128)} %convolution_bitcast_fusion.build_gram_ref), custom_call_target="tpu_custom_call" | custom-call | tf_op jit(solution)/shard_map/pallas_call | solution.py:267
  86.7 1.8 %convolution_bitcast_fusion.2 = f32[1,16,256]{2,1,0:T(8,128)} fusion(f32[16,256]{1,0:T(8,128)} %get-tuple-element.11, f32[256,256]{1,0:T(8,128)} %get-tuple-element.12), kind=kOutput, calls=%fused_computation.2 | convolution fusion | flops 12582912 | bytes 294912 | tf_op jit(solution)/shard_map/dot_general | solution.py:361
Async XLA Ops:
  25.6 11.6 %copy-start = (bf16[8,16,6,256]{3,2,1,0:T(8,128)(2,1)S(1)}, bf16[8,16,6,256]{3,2,1,0:T(8,128)(2,1)}, u32[]{:S(2)}) copy-start(bf16[8,16,6,256]{3,2,1,0:T(8,128)(2,1)} %get-tuple-element.10) | copy-start | bytes 1179652
  25.6 12.6 %copy-start.1 = (bf16[2,16,16,256]{3,2,1,0:T(8,128)(2,1)S(1)}, bf16[2,16,16,256]{3,2,1,0:T(8,128)(2,1)}, u32[]{:S(2)}) copy-start(bf16[2,16,16,256]{3,2,1,0:T(8,128)(2,1)} %get-tuple-element.9) | copy-start | bytes 786436

commit v10 on v9

--- a/solution.py
+++ b/solution.py
@@ -291,7 +291,8 @@
     )(partial, test_gram, build_gram)
 
 
-def mttkrp_kernel(chunk, slot_info, test_ref, build_ref, tile_ref, out_ref, acc_ref):
+def mttkrp_kernel(chunk, n_test_blocks, n_stmt_blocks, slot_tests, slot_builds, slot_stmts,
+                  live_count, test_ref, build_ref, tile_ref, out_ref, acc_ref):
     q = pl.program_id(0)
     c = pl.program_id(1)
     n_chunks = pl.num_programs(1)
@@ -304,7 +305,7 @@
     def _():
         acc_ref[...] = jnp.zeros_like(acc_ref)
 
-    live = q < slot_info[6]
+    live = q < live_count[0]
 
     @pl.when(live)
     def _():
@@ -318,43 +319,49 @@
 
     @pl.when(live & (c == n_chunks - 1))
     def _():
-        rows = pl.ds(pl.multiple_of(slot_info[4 + q] * TILE, TILE), TILE)
+        block = jnp.clip(slot_stmts[q], 0, n_stmt_blocks - 1)
+        rows = pl.ds(pl.multiple_of(block * TILE, TILE), TILE)
         out_ref[rows, :] += acc_ref[...]
 
 
-def local_mttkrp(slot_values, slot_info, test_slab, build_slab):
+def local_mttkrp(slot_values, slot_tests, slot_builds, slot_stmts, live_count, test_slab, build_slab):
     slots, width = slot_values.shape[0], slot_values.shape[1]
     rank = test_slab.shape[1]
     per_block = width // CHUNK
+    n_test_blocks = test_slab.shape[0] // width
+    n_build_blocks = build_slab.shape[0] // width
+
+    def test_map(q, c, tests, builds, stmts, count):
+        return (jnp.clip(tests[q], 0, n_test_blocks - 1) * per_block + c, 0)
+
+    def build_map(q, c, tests, builds, stmts, count):
+        return (jnp.clip(builds[q], 0, n_build_blocks - 1), 0)
+
     grid_spec = pltpu.PrefetchScalarGridSpec(
-        num_scalar_prefetch=1,
+        num_scalar_prefetch=4,
         grid=(slots, per_block),
         in_specs=[
-            pl.BlockSpec((CHUNK, rank), lambda q, c, info: (info[q] * per_block + c, 0)),
-            pl.BlockSpec((width, rank), lambda q, c, info: (info[2 + q], 0)),
-            pl.BlockSpec((None, CHUNK, width, width), lambda q, c, info: (q, c, 0, 0)),
+            pl.BlockSpec((CHUNK, rank), test_map),
+            pl.BlockSpec((width, rank), build_map),
+            pl.BlockSpec((None, CHUNK, width, width), lambda q, c, *info: (q, c, 0, 0)),
         ],
-        out_specs=pl.BlockSpec((SB * width, rank), lambda q, c, info: (0, 0)),
+        out_specs=pl.BlockSpec((SB * width, rank), lambda q, c, *info: (0, 0)),
         scratch_shapes=[pltpu.VMEM((width, rank), jnp.float32)],
     )
     return pl.pallas_call(
-        functools.partial(mttkrp_kernel, CHUNK),
+        functools.partial(mttkrp_kernel, CHUNK, n_test_blocks, SB),
         out_shape=jax.ShapeDtypeStruct((SB * width, rank), jnp.float32),
         grid_spec=grid_spec,
-    )(slot_info, test_slab, build_slab, slot_values)
+    )(slot_tests, slot_builds, slot_stmts, live_count, test_slab, build_slab, slot_values)
 
 
 def shards(tile_values, tile_test, tile_stmt, tile_build, tile_count, test_factor, build_factor):
     test_slab, build_slab = gather_factors(test_factor[0], build_factor[0])
     slot_values = tile_values[0, 0, 0]
     tile_width = slot_values.shape[-1]
-    slot_info = jnp.concatenate([
-        jnp.clip(tile_test[0, 0, 0], 0, test_slab.shape[0] // tile_width - 1),
-        jnp.clip(tile_build[0, 0, 0], 0, build_slab.shape[0] // tile_width - 1),
-        jnp.clip(tile_stmt[0, 0, 0], 0, SB - 1),
-        tile_count[0, 0, 0][None],
-    ]).astype(jnp.int32)
-    running_sum = local_mttkrp(slot_values, slot_info, test_slab, build_slab)
+    running_sum = local_mttkrp(
+        slot_values, tile_test[0, 0, 0], tile_build[0, 0, 0], tile_stmt[0, 0, 0],
+        tile_count[0, 0], test_slab, build_slab)
     slab_test_gram = jnp.dot(test_slab.T, test_slab, preferred_element_type=jnp.float32)
     slab_build_gram = jnp.dot(build_slab.T, build_slab, preferred_element_type=jnp.float32)
     owned_sums, inverse = exchange_and_invert(running_sum, slab_test_gram, slab_build_gram)

time: 88.9 us -> 86.8 us (0.976)
  the two profiles are of different devices: /device:TPU:17 before, /device:TPU:1 now
where the time goes in v10:
time: 86.8 us; the launch traced here: 86.1 us
  Pallas kernels  79.6 us (92%)
  matrix products  3.76 us (4%)
  local copies, waits for them, and re-layouts  2 us (2%)
    pallas_call x1, Pallas kernels, exchange_and_invert(): pl.pallas_call(functools.partial(tail_kernel, n_build, n_test), out_shape...  47.3 us
    pallas_call x1, Pallas kernels, gather_factors(): pl.pallas_call(functools.partial(gather_kernel, n_build, n_test, n_stmt),...  25.3 us
    pallas_call x1, Pallas kernels, local_mttkrp(): pl.pallas_call(functools.partial(mttkrp_kernel, CHUNK, n_test_blocks, SB)...  7.05 us
    reshape x1, local copies, waits for them, and re-layouts, gather_factors(): build_pieces.reshape(-1, build_rows.shape[-1])  1.99 us
    dot_general x1, matrix products, shards(): jnp.dot(owned_sums, inverse, precision=lax.Precision.HIGHEST, preferred_e...  1.8 us

profile of v10, /device:TPU:1, one launch (start us, length us, event | category | flops | bytes accessed | tf_op | source)
XLA Modules:
  0.0 86.1 jit_solution(10559665138326491058)
XLA Ops:
  0.0 25.3 %shard_map.73 = (bf16[2,16,16,256]{3,2,1,0:T(8,128)(2,1)}, bf16[8,16,6,256]{3,2,1,0:T(8,128)(2,1)}) custom-call(bf16[16,256]{1,0:T(8,128)(2,1)} %bitcast.25, bf16[6,256]{1,0:T(8,128)(2,1)} %bitcast.26), custom_call_target="tpu_custom_call" | custom-call | tf_op jit(solution)/shard_map/pallas_call | solution.py:107
  25.3 0.0 copy-start
  25.3 0.0 copy-start.1
  25.3 2.0 %reshape.7.build_ref = bf16[768,256]{1,0:T(8,128)(2,1)} reshape(bf16[8,16,6,256]{3,2,1,0:T(8,128)(2,1)} %get-tuple-element.10) | data formatting | bytes 786432 | tf_op jit(solution)/shard_map/reshape | solution.py:126
  28.0 7.0 %shard_map.74.part_ref = f32[256,256]{1,0:T(8,128)} custom-call(s32[2]{0:T(128)} %bitcast.27, s32[2]{0:T(128)} %bitcast.28, s32[2]{0:T(128)} %bitcast.29, s32[1]{0:T(128)} %bitcast.22.live_count, bf16[512,256]{1,0:T(8,128)(2,1)} %bitcast.24, bf16[768,256]{1,0:T(8,128)(2,1)} %reshape.7.build_ref, bf16[2,128,128,128]{3,2,1,0:T(8,128)(2,1)} %bitcast.23), custom_call_target="tpu_custom_call" | custom-call | tf_op jit(solution)/shard_map/pallas_call | solution.py:351
  35.0 0.0 copy-done
  35.0 1.0 %convolution_bitcast_fusion.build_gram_ref = f32[256,256]{1,0:T(8,128)} fusion(bf16[8,16,6,256]{3,2,1,0:T(8,128)(2,1)S(1)} %copy-done), kind=kOutput, calls=%fused_computation | convolution fusion | flops 100663296 | bytes 655360 | tf_op jit(solution)/shard_map/dot_general | solution.py:366
  36.0 0.0 copy-done.1
  36.0 1.0 %convolution_bitcast_fusion.1.test_gram_ref = f32[256,256]{1,0:T(8,128)} fusion(bf16[2,16,16,256]{3,2,1,0:T(8,128)(2,1)S(1)} %copy-done.1), kind=kOutput, calls=%fused_computation.1 | convolution fusion | flops 67108864 | bytes 524288 | tf_op jit(solution)/shard_map/dot_general | solution.py:365
  37.0 47.3 %shard_map.75 = (f32[16,256]{1,0:T(8,128)}, f32[256,256]{1,0:T(8,128)}) custom-call(f32[256,256]{1,0:T(8,128)} %shard_map.74.part_ref, f32[256,256]{1,0:T(8,128)} %convolution_bitcast_fusion.1.test_gram_ref, f32[256,256]{1,0:T(8,128)} %convolution_bitcast_fusion.build_gram_ref), custom_call_target="tpu_custom_call" | custom-call | tf_op jit(solution)/shard_map/pallas_call | solution.py:267
  84.3 1.8 %convolution_bitcast_fusion.2 = f32[1,16,256]{2,1,0:T(8,128)} fusion(f32[16,256]{1,0:T(8,128)} %get-tuple-element.11, f32[256,256]{1,0:T(8,128)} %get-tuple-element.12), kind=kOutput, calls=%fused_computation.2 | convolution fusion | flops 12582912 | bytes 294912 | tf_op jit(solution)/shard_map/dot_general | solution.py:368
Async XLA Ops:
  25.3 9.7 %copy-start = (bf16[8,16,6,256]{3,2,1,0:T(8,128)(2,1)S(1)}, bf16[8,16,6,256]{3,2,1,0:T(8,128)(2,1)}, u32[]{:S(2)}) copy-start(bf16[8,16,6,256]{3,2,1,0:T(8,128)(2,1)} %get-tuple-element.10) | copy-start | bytes 1179652
  25.3 10.7 %copy-start.1 = (bf16[2,16,16,256]{3,2,1,0:T(8,128)(2,1)S(1)}, bf16[2,16,16,256]{3,2,1,0:T(8,128)(2,1)}, u32[]{:S(2)}) copy-start(bf16[2,16,16,256]{3,2,1,0:T(8,128)(2,1)} %get-tuple-element.9) | copy-start | bytes 786436

commit v11 on v10

--- a/solution.py
+++ b/solution.py
@@ -146,7 +146,7 @@
         a_ref[pl.ds(k, 1), :] = jnp.where(is_k, -inv, row * inv)
         return next_row
 
-    lax.fori_loop(0, n, step, a_ref[0:1, :], unroll=8)
+    lax.fori_loop(0, n, step, a_ref[0:1, :], unroll=16)
     a_ref[...] = -a_ref[...]
 
 
@@ -358,7 +358,6 @@
 def shards(tile_values, tile_test, tile_stmt, tile_build, tile_count, test_factor, build_factor):
     test_slab, build_slab = gather_factors(test_factor[0], build_factor[0])
     slot_values = tile_values[0, 0, 0]
-    tile_width = slot_values.shape[-1]
     running_sum = local_mttkrp(
         slot_values, tile_test[0, 0, 0], tile_build[0, 0, 0], tile_stmt[0, 0, 0],
         tile_count[0, 0], test_slab, build_slab)

time: 86.8 us -> 84.4 us (0.972)
  Pallas kernels: 79.6 us -> 77.1 us
    pallas_call x1, Pallas kernels: 47.3 us -> 42.9 us  [exchange_and_invert(): pl.pallas_call(functools.partial(tail_kernel, n_build, n_test), out_shape...]
    pallas_call x1, Pallas kernels: 7.05 us -> 8.98 us  [local_mttkrp(): pl.pallas_call(functools.partial(mttkrp_kernel, CHUNK, n_test_blocks, SB)...]
where the time goes in v11:
time: 84.4 us; the launch traced here: 83.6 us
  Pallas kernels  77.1 us (91%)
  matrix products  3.77 us (4%)
  local copies, waits for them, and re-layouts  2 us (2%)
    pallas_call x1, Pallas kernels, exchange_and_invert(): pl.pallas_call(functools.partial(tail_kernel, n_build, n_test), out_shape...  42.9 us
    pallas_call x1, Pallas kernels, gather_factors(): pl.pallas_call(functools.partial(gather_kernel, n_build, n_test, n_stmt),...  25.3 us
    pallas_call x1, Pallas kernels, local_mttkrp(): pl.pallas_call(functools.partial(mttkrp_kernel, CHUNK, n_test_blocks, SB)...  8.98 us
    reshape x1, local copies, waits for them, and re-layouts, gather_factors(): build_pieces.reshape(-1, build_rows.shape[-1])  1.99 us
    dot_general x1, matrix products, shards(): jnp.dot(owned_sums, inverse, precision=lax.Precision.HIGHEST, preferred_e...  1.8 us

profile of v11, /device:TPU:1, one launch (start us, length us, event | category | flops | bytes accessed | tf_op | source)
XLA Modules:
  0.0 83.6 jit_solution(5695472559979992502)
XLA Ops:
  0.0 25.3 %shard_map.73 = (bf16[2,16,16,256]{3,2,1,0:T(8,128)(2,1)}, bf16[8,16,6,256]{3,2,1,0:T(8,128)(2,1)}) custom-call(bf16[16,256]{1,0:T(8,128)(2,1)} %bitcast.25, bf16[6,256]{1,0:T(8,128)(2,1)} %bitcast.26), custom_call_target="tpu_custom_call" | custom-call | tf_op jit(solution)/shard_map/pallas_call | solution.py:107
  25.3 0.0 copy-start
  25.3 0.0 copy-start.1
  25.3 2.0 %reshape.7.build_ref = bf16[768,256]{1,0:T(8,128)(2,1)} reshape(bf16[8,16,6,256]{3,2,1,0:T(8,128)(2,1)} %get-tuple-element.10) | data formatting | bytes 786432 | tf_op jit(solution)/shard_map/reshape | solution.py:126
  28.0 9.0 %shard_map.74.part_ref = f32[256,256]{1,0:T(8,128)} custom-call(s32[2]{0:T(128)} %bitcast.27, s32[2]{0:T(128)} %bitcast.28, s32[2]{0:T(128)} %bitcast.29, s32[1]{0:T(128)} %bitcast.22.live_count, bf16[512,256]{1,0:T(8,128)(2,1)} %bitcast.24, bf16[768,256]{1,0:T(8,128)(2,1)} %reshape.7.build_ref, bf16[2,128,128,128]{3,2,1,0:T(8,128)(2,1)} %bitcast.23), custom_call_target="tpu_custom_call" | custom-call | tf_op jit(solution)/shard_map/pallas_call | solution.py:351
  36.9 0.0 copy-done
  37.0 1.0 %convolution_bitcast_fusion.build_gram_ref = f32[256,256]{1,0:T(8,128)} fusion(bf16[8,16,6,256]{3,2,1,0:T(8,128)(2,1)S(1)} %copy-done), kind=kOutput, calls=%fused_computation | convolution fusion | flops 100663296 | bytes 655360 | tf_op jit(solution)/shard_map/dot_general | solution.py:365
  38.0 0.0 copy-done.1
  38.0 1.0 %convolution_bitcast_fusion.1.test_gram_ref = f32[256,256]{1,0:T(8,128)} fusion(bf16[2,16,16,256]{3,2,1,0:T(8,128)(2,1)S(1)} %copy-done.1), kind=kOutput, calls=%fused_computation.1 | convolution fusion | flops 67108864 | bytes 524288 | tf_op jit(solution)/shard_map/dot_general | solution.py:364
  38.9 42.9 %shard_map.75 = (f32[16,256]{1,0:T(8,128)}, f32[256,256]{1,0:T(8,128)}) custom-call(f32[256,256]{1,0:T(8,128)} %shard_map.74.part_ref, f32[256,256]{1,0:T(8,128)} %convolution_bitcast_fusion.1.test_gram_ref, f32[256,256]{1,0:T(8,128)} %convolution_bitcast_fusion.build_gram_ref), custom_call_target="tpu_custom_call" | custom-call | tf_op jit(solution)/shard_map/pallas_call | solution.py:267
  81.8 1.8 %convolution_bitcast_fusion.2 = f32[1,16,256]{2,1,0:T(8,128)} fusion(f32[16,256]{1,0:T(8,128)} %get-tuple-element.11, f32[256,256]{1,0:T(8,128)} %get-tuple-element.12), kind=kOutput, calls=%fused_computation.2 | convolution fusion | flops 12582912 | bytes 294912 | tf_op jit(solution)/shard_map/dot_general | solution.py:367
Async XLA Ops:
  25.3 11.6 %copy-start = (bf16[8,16,6,256]{3,2,1,0:T(8,128)(2,1)S(1)}, bf16[8,16,6,256]{3,2,1,0:T(8,128)(2,1)}, u32[]{:S(2)}) copy-start(bf16[8,16,6,256]{3,2,1,0:T(8,128)(2,1)} %get-tuple-element.10) | copy-start | bytes 1179652
  25.3 12.6 %copy-start.1 = (bf16[2,16,16,256]{3,2,1,0:T(8,128)(2,1)S(1)}, bf16[2,16,16,256]{3,2,1,0:T(8,128)(2,1)}, u32[]{:S(2)}) copy-start(bf16[2,16,16,256]{3,2,1,0:T(8,128)(2,1)} %get-tuple-element.9) | copy-start | bytes 786436

commit v12 on v11

--- a/solution.py
+++ b/solution.py
@@ -146,7 +146,7 @@
         a_ref[pl.ds(k, 1), :] = jnp.where(is_k, -inv, row * inv)
         return next_row
 
-    lax.fori_loop(0, n, step, a_ref[0:1, :], unroll=16)
+    lax.fori_loop(0, n, step, a_ref[0:1, :], unroll=32)
     a_ref[...] = -a_ref[...]
 
 

time: 84.4 us -> 82.7 us (0.980)
  Pallas kernels: 77.1 us -> 75.3 us
    pallas_call x1, Pallas kernels: 8.98 us -> 7.05 us  [local_mttkrp(): pl.pallas_call(functools.partial(mttkrp_kernel, CHUNK, n_test_blocks, SB)...]
where the time goes in v12:
time: 82.7 us; the launch traced here: 81.8 us
  Pallas kernels  75.3 us (91%)
  matrix products  3.76 us (5%)
  local copies, waits for them, and re-layouts  2 us (2%)
    pallas_call x1, Pallas kernels, exchange_and_invert(): pl.pallas_call(functools.partial(tail_kernel, n_build, n_test), out_shape...  43 us
    pallas_call x1, Pallas kernels, gather_factors(): pl.pallas_call(functools.partial(gather_kernel, n_build, n_test, n_stmt),...  25.3 us
    pallas_call x1, Pallas kernels, local_mttkrp(): pl.pallas_call(functools.partial(mttkrp_kernel, CHUNK, n_test_blocks, SB)...  7.05 us
    reshape x1, local copies, waits for them, and re-layouts, gather_factors(): build_pieces.reshape(-1, build_rows.shape[-1])  1.99 us
    dot_general x1, matrix products, shards(): jnp.dot(owned_sums, inverse, precision=lax.Precision.HIGHEST, preferred_e...  1.8 us

profile of v12, /device:TPU:1, one launch (start us, length us, event | category | flops | bytes accessed | tf_op | source)
XLA Modules:
  0.0 81.8 jit_solution(16969319579171129884)
XLA Ops:
  0.0 25.3 %shard_map.73 = (bf16[2,16,16,256]{3,2,1,0:T(8,128)(2,1)}, bf16[8,16,6,256]{3,2,1,0:T(8,128)(2,1)}) custom-call(bf16[16,256]{1,0:T(8,128)(2,1)} %bitcast.25, bf16[6,256]{1,0:T(8,128)(2,1)} %bitcast.26), custom_call_target="tpu_custom_call" | custom-call | tf_op jit(solution)/shard_map/pallas_call | solution.py:107
  25.3 0.0 copy-start
  25.3 0.0 copy-start.1
  25.3 2.0 %reshape.7.build_ref = bf16[768,256]{1,0:T(8,128)(2,1)} reshape(bf16[8,16,6,256]{3,2,1,0:T(8,128)(2,1)} %get-tuple-element.10) | data formatting | bytes 786432 | tf_op jit(solution)/shard_map/reshape | solution.py:126
  28.0 7.0 %shard_map.74.part_ref = f32[256,256]{1,0:T(8,128)} custom-call(s32[2]{0:T(128)} %bitcast.27, s32[2]{0:T(128)} %bitcast.28, s32[2]{0:T(128)} %bitcast.29, s32[1]{0:T(128)} %bitcast.22.live_count, bf16[512,256]{1,0:T(8,128)(2,1)} %bitcast.24, bf16[768,256]{1,0:T(8,128)(2,1)} %reshape.7.build_ref, bf16[2,128,128,128]{3,2,1,0:T(8,128)(2,1)} %bitcast.23), custom_call_target="tpu_custom_call" | custom-call | tf_op jit(solution)/shard_map/pallas_call | solution.py:351
  35.0 0.0 copy-done
  35.0 1.0 %convolution_bitcast_fusion.build_gram_ref = f32[256,256]{1,0:T(8,128)} fusion(bf16[8,16,6,256]{3,2,1,0:T(8,128)(2,1)S(1)} %copy-done), kind=kOutput, calls=%fused_computation | convolution fusion | flops 100663296 | bytes 655360 | tf_op jit(solution)/shard_map/dot_general | solution.py:365
  36.0 0.0 copy-done.1
  36.0 1.0 %convolution_bitcast_fusion.1.test_gram_ref = f32[256,256]{1,0:T(8,128)} fusion(bf16[2,16,16,256]{3,2,1,0:T(8,128)(2,1)S(1)} %copy-done.1), kind=kOutput, calls=%fused_computation.1 | convolution fusion | flops 67108864 | bytes 524288 | tf_op jit(solution)/shard_map/dot_general | solution.py:364
  37.0 43.0 %shard_map.75 = (f32[16,256]{1,0:T(8,128)}, f32[256,256]{1,0:T(8,128)}) custom-call(f32[256,256]{1,0:T(8,128)} %shard_map.74.part_ref, f32[256,256]{1,0:T(8,128)} %convolution_bitcast_fusion.1.test_gram_ref, f32[256,256]{1,0:T(8,128)} %convolution_bitcast_fusion.build_gram_ref), custom_call_target="tpu_custom_call" | custom-call | tf_op jit(solution)/shard_map/pallas_call | solution.py:267
  80.0 1.8 %convolution_bitcast_fusion.2 = f32[1,16,256]{2,1,0:T(8,128)} fusion(f32[16,256]{1,0:T(8,128)} %get-tuple-element.11, f32[256,256]{1,0:T(8,128)} %get-tuple-element.12), kind=kOutput, calls=%fused_computation.2 | convolution fusion | flops 12582912 | bytes 294912 | tf_op jit(solution)/shard_map/dot_general | solution.py:367
Async XLA Ops:
  25.3 9.7 %copy-start = (bf16[8,16,6,256]{3,2,1,0:T(8,128)(2,1)S(1)}, bf16[8,16,6,256]{3,2,1,0:T(8,128)(2,1)}, u32[]{:S(2)}) copy-start(bf16[8,16,6,256]{3,2,1,0:T(8,128)(2,1)} %get-tuple-element.10) | copy-start | bytes 1179652
  25.3 10.7 %copy-start.1 = (bf16[2,16,16,256]{3,2,1,0:T(8,128)(2,1)S(1)}, bf16[2,16,16,256]{3,2,1,0:T(8,128)(2,1)}, u32[]{:S(2)}) copy-start(bf16[2,16,16,256]{3,2,1,0:T(8,128)(2,1)} %get-tuple-element.9) | copy-start | bytes 786436

commit v13 on v12

--- a/solution.py
+++ b/solution.py
@@ -146,7 +146,7 @@
         a_ref[pl.ds(k, 1), :] = jnp.where(is_k, -inv, row * inv)
         return next_row
 
-    lax.fori_loop(0, n, step, a_ref[0:1, :], unroll=32)
+    lax.fori_loop(0, n, step, a_ref[0:1, :], unroll=64)
     a_ref[...] = -a_ref[...]
 
 

time: 82.7 us -> 82.1 us (level)
  no operation moved by 1% of the time
where the time goes in v13:
time: 82.1 us; the launch traced here: 81.1 us
  Pallas kernels  74.6 us (91%)
  matrix products  3.76 us (5%)
  local copies, waits for them, and re-layouts  2 us (2%)
    pallas_call x1, Pallas kernels, exchange_and_invert(): pl.pallas_call(functools.partial(tail_kernel, n_build, n_test), out_shape...  42.3 us
    pallas_call x1, Pallas kernels, gather_factors(): pl.pallas_call(functools.partial(gather_kernel, n_build, n_test, n_stmt),...  25.3 us
    pallas_call x1, Pallas kernels, local_mttkrp(): pl.pallas_call(functools.partial(mttkrp_kernel, CHUNK, n_test_blocks, SB)...  7.05 us
    reshape x1, local copies, waits for them, and re-layouts, gather_factors(): build_pieces.reshape(-1, build_rows.shape[-1])  1.99 us
    dot_general x1, matrix products, shards(): jnp.dot(owned_sums, inverse, precision=lax.Precision.HIGHEST, preferred_e...  1.8 us

profile of v13, /device:TPU:1, one launch (start us, length us, event | category | flops | bytes accessed | tf_op | source)
XLA Modules:
  0.0 81.1 jit_solution(14572655880036511053)
XLA Ops:
  0.0 25.3 %shard_map.73 = (bf16[2,16,16,256]{3,2,1,0:T(8,128)(2,1)}, bf16[8,16,6,256]{3,2,1,0:T(8,128)(2,1)}) custom-call(bf16[16,256]{1,0:T(8,128)(2,1)} %bitcast.25, bf16[6,256]{1,0:T(8,128)(2,1)} %bitcast.26), custom_call_target="tpu_custom_call" | custom-call | tf_op jit(solution)/shard_map/pallas_call | solution.py:107
  25.3 0.0 copy-start
  25.3 0.0 copy-start.1
  25.3 2.0 %reshape.7.build_ref = bf16[768,256]{1,0:T(8,128)(2,1)} reshape(bf16[8,16,6,256]{3,2,1,0:T(8,128)(2,1)} %get-tuple-element.10) | data formatting | bytes 786432 | tf_op jit(solution)/shard_map/reshape | solution.py:126
  28.0 7.0 %shard_map.74.part_ref = f32[256,256]{1,0:T(8,128)} custom-call(s32[2]{0:T(128)} %bitcast.27, s32[2]{0:T(128)} %bitcast.28, s32[2]{0:T(128)} %bitcast.29, s32[1]{0:T(128)} %bitcast.22.live_count, bf16[512,256]{1,0:T(8,128)(2,1)} %bitcast.24, bf16[768,256]{1,0:T(8,128)(2,1)} %reshape.7.build_ref, bf16[2,128,128,128]{3,2,1,0:T(8,128)(2,1)} %bitcast.23), custom_call_target="tpu_custom_call" | custom-call | tf_op jit(solution)/shard_map/pallas_call | solution.py:351
  35.0 0.0 copy-done
  35.0 1.0 %convolution_bitcast_fusion.build_gram_ref = f32[256,256]{1,0:T(8,128)} fusion(bf16[8,16,6,256]{3,2,1,0:T(8,128)(2,1)S(1)} %copy-done), kind=kOutput, calls=%fused_computation | convolution fusion | flops 100663296 | bytes 655360 | tf_op jit(solution)/shard_map/dot_general | solution.py:365
  36.0 0.0 copy-done.1
  36.0 1.0 %convolution_bitcast_fusion.1.test_gram_ref = f32[256,256]{1,0:T(8,128)} fusion(bf16[2,16,16,256]{3,2,1,0:T(8,128)(2,1)S(1)} %copy-done.1), kind=kOutput, calls=%fused_computation.1 | convolution fusion | flops 67108864 | bytes 524288 | tf_op jit(solution)/shard_map/dot_general | solution.py:364
  37.0 42.3 %shard_map.75 = (f32[16,256]{1,0:T(8,128)}, f32[256,256]{1,0:T(8,128)}) custom-call(f32[256,256]{1,0:T(8,128)} %shard_map.74.part_ref, f32[256,256]{1,0:T(8,128)} %convolution_bitcast_fusion.1.test_gram_ref, f32[256,256]{1,0:T(8,128)} %convolution_bitcast_fusion.build_gram_ref), custom_call_target="tpu_custom_call" | custom-call | tf_op jit(solution)/shard_map/pallas_call | solution.py:267
  79.3 1.8 %convolution_bitcast_fusion.2 = f32[1,16,256]{2,1,0:T(8,128)} fusion(f32[16,256]{1,0:T(8,128)} %get-tuple-element.11, f32[256,256]{1,0:T(8,128)} %get-tuple-element.12), kind=kOutput, calls=%fused_computation.2 | convolution fusion | flops 12582912 | bytes 294912 | tf_op jit(solution)/shard_map/dot_general | solution.py:367
Async XLA Ops:
  25.3 9.7 %copy-start = (bf16[8,16,6,256]{3,2,1,0:T(8,128)(2,1)S(1)}, bf16[8,16,6,256]{3,2,1,0:T(8,128)(2,1)}, u32[]{:S(2)}) copy-start(bf16[8,16,6,256]{3,2,1,0:T(8,128)(2,1)} %get-tuple-element.10) | copy-start | bytes 1179652
  25.3 10.7 %copy-start.1 = (bf16[2,16,16,256]{3,2,1,0:T(8,128)(2,1)S(1)}, bf16[2,16,16,256]{3,2,1,0:T(8,128)(2,1)}, u32[]{:S(2)}) copy-start(bf16[2,16,16,256]{3,2,1,0:T(8,128)(2,1)} %get-tuple-element.9) | copy-start | bytes 786436

commit v14 on v13

--- a/solution.py
+++ b/solution.py
@@ -146,7 +146,7 @@
         a_ref[pl.ds(k, 1), :] = jnp.where(is_k, -inv, row * inv)
         return next_row
 
-    lax.fori_loop(0, n, step, a_ref[0:1, :], unroll=64)
+    lax.fori_loop(0, n, step, a_ref[0:1, :], unroll=128)
     a_ref[...] = -a_ref[...]
 
 

time: 82.1 us -> 81.6 us (level)
  no operation moved by 1% of the time
where the time goes in v14:
time: 81.6 us; the launch traced here: 80.6 us
  Pallas kernels  74.1 us (91%)
  matrix products  3.76 us (5%)
  local copies, waits for them, and re-layouts  2 us (2%)
    pallas_call x1, Pallas kernels, exchange_and_invert(): pl.pallas_call(functools.partial(tail_kernel, n_build, n_test), out_shape...  41.8 us
    pallas_call x1, Pallas kernels, gather_factors(): pl.pallas_call(functools.partial(gather_kernel, n_build, n_test, n_stmt),...  25.3 us
    pallas_call x1, Pallas kernels, local_mttkrp(): pl.pallas_call(functools.partial(mttkrp_kernel, CHUNK, n_test_blocks, SB)...  7.05 us
    reshape x1, local copies, waits for them, and re-layouts, gather_factors(): build_pieces.reshape(-1, build_rows.shape[-1])  1.99 us
    dot_general x1, matrix products, shards(): jnp.dot(owned_sums, inverse, precision=lax.Precision.HIGHEST, preferred_e...  1.8 us

profile of v14, /device:TPU:1, one launch (start us, length us, event | category | flops | bytes accessed | tf_op | source)
XLA Modules:
  0.0 80.6 jit_solution(11976901188436785481)
XLA Ops:
  0.0 25.3 %shard_map.73 = (bf16[2,16,16,256]{3,2,1,0:T(8,128)(2,1)}, bf16[8,16,6,256]{3,2,1,0:T(8,128)(2,1)}) custom-call(bf16[16,256]{1,0:T(8,128)(2,1)} %bitcast.25, bf16[6,256]{1,0:T(8,128)(2,1)} %bitcast.26), custom_call_target="tpu_custom_call" | custom-call | tf_op jit(solution)/shard_map/pallas_call | solution.py:107
  25.3 0.0 copy-start
  25.3 0.0 copy-start.1
  25.3 2.0 %reshape.7.build_ref = bf16[768,256]{1,0:T(8,128)(2,1)} reshape(bf16[8,16,6,256]{3,2,1,0:T(8,128)(2,1)} %get-tuple-element.10) | data formatting | bytes 786432 | tf_op jit(solution)/shard_map/reshape | solution.py:126
  28.0 7.0 %shard_map.74.part_ref = f32[256,256]{1,0:T(8,128)} custom-call(s32[2]{0:T(128)} %bitcast.27, s32[2]{0:T(128)} %bitcast.28, s32[2]{0:T(128)} %bitcast.29, s32[1]{0:T(128)} %bitcast.22.live_count, bf16[512,256]{1,0:T(8,128)(2,1)} %bitcast.24, bf16[768,256]{1,0:T(8,128)(2,1)} %reshape.7.build_ref, bf16[2,128,128,128]{3,2,1,0:T(8,128)(2,1)} %bitcast.23), custom_call_target="tpu_custom_call" | custom-call | tf_op jit(solution)/shard_map/pallas_call | solution.py:351
  35.0 0.0 copy-done
  35.0 1.0 %convolution_bitcast_fusion.build_gram_ref = f32[256,256]{1,0:T(8,128)} fusion(bf16[8,16,6,256]{3,2,1,0:T(8,128)(2,1)S(1)} %copy-done), kind=kOutput, calls=%fused_computation | convolution fusion | flops 100663296 | bytes 655360 | tf_op jit(solution)/shard_map/dot_general | solution.py:365
  36.0 0.0 copy-done.1
  36.0 1.0 %convolution_bitcast_fusion.1.test_gram_ref = f32[256,256]{1,0:T(8,128)} fusion(bf16[2,16,16,256]{3,2,1,0:T(8,128)(2,1)S(1)} %copy-done.1), kind=kOutput, calls=%fused_computation.1 | convolution fusion | flops 67108864 | bytes 524288 | tf_op jit(solution)/shard_map/dot_general | solution.py:364
  37.0 41.8 %shard_map.75 = (f32[16,256]{1,0:T(8,128)}, f32[256,256]{1,0:T(8,128)}) custom-call(f32[256,256]{1,0:T(8,128)} %shard_map.74.part_ref, f32[256,256]{1,0:T(8,128)} %convolution_bitcast_fusion.1.test_gram_ref, f32[256,256]{1,0:T(8,128)} %convolution_bitcast_fusion.build_gram_ref), custom_call_target="tpu_custom_call" | custom-call | tf_op jit(solution)/shard_map/pallas_call | solution.py:267
  78.8 1.8 %convolution_bitcast_fusion.2 = f32[1,16,256]{2,1,0:T(8,128)} fusion(f32[16,256]{1,0:T(8,128)} %get-tuple-element.11, f32[256,256]{1,0:T(8,128)} %get-tuple-element.12), kind=kOutput, calls=%fused_computation.2 | convolution fusion | flops 12582912 | bytes 294912 | tf_op jit(solution)/shard_map/dot_general | solution.py:367
Async XLA Ops:
  25.3 9.7 %copy-start = (bf16[8,16,6,256]{3,2,1,0:T(8,128)(2,1)S(1)}, bf16[8,16,6,256]{3,2,1,0:T(8,128)(2,1)}, u32[]{:S(2)}) copy-start(bf16[8,16,6,256]{3,2,1,0:T(8,128)(2,1)} %get-tuple-element.10) | copy-start | bytes 1179652
  25.3 10.7 %copy-start.1 = (bf16[2,16,16,256]{3,2,1,0:T(8,128)(2,1)S(1)}, bf16[2,16,16,256]{3,2,1,0:T(8,128)(2,1)}, u32[]{:S(2)}) copy-start(bf16[2,16,16,256]{3,2,1,0:T(8,128)(2,1)} %get-tuple-element.9) | copy-start | bytes 786436

commit v15 on v14

--- a/solution.py
+++ b/solution.py
@@ -10,7 +10,7 @@
 TILE = 128
 SB = 2
 MESH = pl.DeviceIdType.MESH
-CHUNK = 32
+CHUNK = 64
 
 
 def gather_kernel(n_build, n_test, n_stmt, test_in, build_in, test_out, build_out,

time: 81.6 us -> 80 us (0.980)
  Pallas kernels: 74.1 us -> 72.9 us
    pallas_call x1, Pallas kernels: 7.05 us -> 5.51 us  [local_mttkrp(): pl.pallas_call(functools.partial(mttkrp_kernel, CHUNK, n_test_blocks, SB)...]
where the time goes in v15:
time: 80 us; the launch traced here: 79.3 us
  Pallas kernels  72.9 us (91%)
  matrix products  3.76 us (5%)
  local copies, waits for them, and re-layouts  2 us (2%)
    pallas_call x1, Pallas kernels, exchange_and_invert(): pl.pallas_call(functools.partial(tail_kernel, n_build, n_test), out_shape...  42.1 us
    pallas_call x1, Pallas kernels, gather_factors(): pl.pallas_call(functools.partial(gather_kernel, n_build, n_test, n_stmt),...  25.3 us
    pallas_call x1, Pallas kernels, local_mttkrp(): pl.pallas_call(functools.partial(mttkrp_kernel, CHUNK, n_test_blocks, SB)...  5.51 us
    reshape x1, local copies, waits for them, and re-layouts, gather_factors(): build_pieces.reshape(-1, build_rows.shape[-1])  1.99 us
    dot_general x1, matrix products, shards(): jnp.dot(owned_sums, inverse, precision=lax.Precision.HIGHEST, preferred_e...  1.8 us

profile of v15, /device:TPU:1, one launch (start us, length us, event | category | flops | bytes accessed | tf_op | source)
XLA Modules:
  0.0 79.3 jit_solution(15232879775803972703)
XLA Ops:
  0.0 25.3 %shard_map.73 = (bf16[2,16,16,256]{3,2,1,0:T(8,128)(2,1)}, bf16[8,16,6,256]{3,2,1,0:T(8,128)(2,1)}) custom-call(bf16[16,256]{1,0:T(8,128)(2,1)} %bitcast.25, bf16[6,256]{1,0:T(8,128)(2,1)} %bitcast.26), custom_call_target="tpu_custom_call" | custom-call | tf_op jit(solution)/shard_map/pallas_call | solution.py:107
  25.3 0.0 copy-start
  25.3 0.0 copy-start.1
  25.3 2.0 %reshape.7.build_ref = bf16[768,256]{1,0:T(8,128)(2,1)} reshape(bf16[8,16,6,256]{3,2,1,0:T(8,128)(2,1)} %get-tuple-element.10) | data formatting | bytes 786432 | tf_op jit(solution)/shard_map/reshape | solution.py:126
  28.0 5.5 %shard_map.74.part_ref = f32[256,256]{1,0:T(8,128)} custom-call(s32[2]{0:T(128)} %bitcast.27, s32[2]{0:T(128)} %bitcast.28, s32[2]{0:T(128)} %bitcast.29, s32[1]{0:T(128)} %bitcast.22.live_count, bf16[512,256]{1,0:T(8,128)(2,1)} %bitcast.24, bf16[768,256]{1,0:T(8,128)(2,1)} %reshape.7.build_ref, bf16[2,128,128,128]{3,2,1,0:T(8,128)(2,1)} %bitcast.23), custom_call_target="tpu_custom_call" | custom-call | tf_op jit(solution)/shard_map/pallas_call | solution.py:351
  33.5 0.0 copy-done
  33.5 1.0 %convolution_bitcast_fusion.build_gram_ref = f32[256,256]{1,0:T(8,128)} fusion(bf16[8,16,6,256]{3,2,1,0:T(8,128)(2,1)S(1)} %copy-done), kind=kOutput, calls=%fused_computation | convolution fusion | flops 100663296 | bytes 655360 | tf_op jit(solution)/shard_map/dot_general | solution.py:365
  34.5 0.0 copy-done.1
  34.5 1.0 %convolution_bitcast_fusion.1.test_gram_ref = f32[256,256]{1,0:T(8,128)} fusion(bf16[2,16,16,256]{3,2,1,0:T(8,128)(2,1)S(1)} %copy-done.1), kind=kOutput, calls=%fused_computation.1 | convolution fusion | flops 67108864 | bytes 524288 | tf_op jit(solution)/shard_map/dot_general | solution.py:364
  35.4 42.1 %shard_map.75 = (f32[16,256]{1,0:T(8,128)}, f32[256,256]{1,0:T(8,128)}) custom-call(f32[256,256]{1,0:T(8,128)} %shard_map.74.part_ref, f32[256,256]{1,0:T(8,128)} %convolution_bitcast_fusion.1.test_gram_ref, f32[256,256]{1,0:T(8,128)} %convolution_bitcast_fusion.build_gram_ref), custom_call_target="tpu_custom_call" | custom-call | tf_op jit(solution)/shard_map/pallas_call | solution.py:267
  77.5 1.8 %convolution_bitcast_fusion.2 = f32[1,16,256]{2,1,0:T(8,128)} fusion(f32[16,256]{1,0:T(8,128)} %get-tuple-element.11, f32[256,256]{1,0:T(8,128)} %get-tuple-element.12), kind=kOutput, calls=%fused_computation.2 | convolution fusion | flops 12582912 | bytes 294912 | tf_op jit(solution)/shard_map/dot_general | solution.py:367
Async XLA Ops:
  25.3 8.2 %copy-start = (bf16[8,16,6,256]{3,2,1,0:T(8,128)(2,1)S(1)}, bf16[8,16,6,256]{3,2,1,0:T(8,128)(2,1)}, u32[]{:S(2)}) copy-start(bf16[8,16,6,256]{3,2,1,0:T(8,128)(2,1)} %get-tuple-element.10) | copy-start | bytes 1179652
  25.3 9.2 %copy-start.1 = (bf16[2,16,16,256]{3,2,1,0:T(8,128)(2,1)S(1)}, bf16[2,16,16,256]{3,2,1,0:T(8,128)(2,1)}, u32[]{:S(2)}) copy-start(bf16[2,16,16,256]{3,2,1,0:T(8,128)(2,1)} %get-tuple-element.9) | copy-start | bytes 786436

commit v16 on v15

--- a/solution.py
+++ b/solution.py
@@ -10,7 +10,7 @@
 TILE = 128
 SB = 2
 MESH = pl.DeviceIdType.MESH
-CHUNK = 64
+CHUNK = 128
 
 
 def gather_kernel(n_build, n_test, n_stmt, test_in, build_in, test_out, build_out,

time: 80 us -> 79.6 us (level)
    pallas_call x1, Pallas kernels: 42.1 us -> 38.8 us  [exchange_and_invert(): pl.pallas_call(functools.partial(tail_kernel, n_build, n_test), out_shape...]
    pallas_call x1, Pallas kernels: 5.51 us -> 8.43 us  [local_mttkrp(): pl.pallas_call(functools.partial(mttkrp_kernel, CHUNK, n_test_blocks, SB)...]
where the time goes in v16:
time: 79.6 us; the launch traced here: 79 us
  Pallas kernels  72.6 us (91%)
  matrix products  3.76 us (5%)
  local copies, waits for them, and re-layouts  2 us (3%)
    pallas_call x1, Pallas kernels, exchange_and_invert(): pl.pallas_call(functools.partial(tail_kernel, n_build, n_test), out_shape...  38.8 us
    pallas_call x1, Pallas kernels, gather_factors(): pl.pallas_call(functools.partial(gather_kernel, n_build, n_test, n_stmt),...  25.3 us
    pallas_call x1, Pallas kernels, local_mttkrp(): pl.pallas_call(functools.partial(mttkrp_kernel, CHUNK, n_test_blocks, SB)...  8.43 us
    reshape x1, local copies, waits for them, and re-layouts, gather_factors(): build_pieces.reshape(-1, build_rows.shape[-1])  1.99 us
    dot_general x1, matrix products, shards(): jnp.dot(owned_sums, inverse, precision=lax.Precision.HIGHEST, preferred_e...  1.8 us

profile of v16, /device:TPU:1, one launch (start us, length us, event | category | flops | bytes accessed | tf_op | source)
XLA Modules:
  0.0 79.0 jit_solution(7617854568050023230)
XLA Ops:
  0.0 25.3 %shard_map.73 = (bf16[2,16,16,256]{3,2,1,0:T(8,128)(2,1)}, bf16[8,16,6,256]{3,2,1,0:T(8,128)(2,1)}) custom-call(bf16[16,256]{1,0:T(8,128)(2,1)} %bitcast.25, bf16[6,256]{1,0:T(8,128)(2,1)} %bitcast.26), custom_call_target="tpu_custom_call" | custom-call | tf_op jit(solution)/shard_map/pallas_call | solution.py:107
  25.3 0.0 copy-start
  25.3 0.0 copy-start.1
  25.3 2.0 %reshape.7.build_ref = bf16[768,256]{1,0:T(8,128)(2,1)} reshape(bf16[8,16,6,256]{3,2,1,0:T(8,128)(2,1)} %get-tuple-element.10) | data formatting | bytes 786432 | tf_op jit(solution)/shard_map/reshape | solution.py:126
  28.0 8.4 %shard_map.74.part_ref = f32[256,256]{1,0:T(8,128)} custom-call(s32[2]{0:T(128)} %bitcast.27, s32[2]{0:T(128)} %bitcast.28, s32[2]{0:T(128)} %bitcast.29, s32[1]{0:T(128)} %bitcast.22.live_count, bf16[512,256]{1,0:T(8,128)(2,1)} %bitcast.24, bf16[768,256]{1,0:T(8,128)(2,1)} %reshape.7.build_ref, bf16[2,128,128,128]{3,2,1,0:T(8,128)(2,1)} %bitcast.23), custom_call_target="tpu_custom_call" | custom-call | tf_op jit(solution)/shard_map/pallas_call | solution.py:351
  36.4 0.0 copy-done
  36.4 1.0 %convolution_bitcast_fusion.build_gram_ref = f32[256,256]{1,0:T(8,128)} fusion(bf16[8,16,6,256]{3,2,1,0:T(8,128)(2,1)S(1)} %copy-done), kind=kOutput, calls=%fused_computation | convolution fusion | flops 100663296 | bytes 655360 | tf_op jit(solution)/shard_map/dot_general | solution.py:365
  37.4 0.0 copy-done.1
  37.4 1.0 %convolution_bitcast_fusion.1.test_gram_ref = f32[256,256]{1,0:T(8,128)} fusion(bf16[2,16,16,256]{3,2,1,0:T(8,128)(2,1)S(1)} %copy-done.1), kind=kOutput, calls=%fused_computation.1 | convolution fusion | flops 67108864 | bytes 524288 | tf_op jit(solution)/shard_map/dot_general | solution.py:364
  38.4 38.8 %shard_map.75 = (f32[16,256]{1,0:T(8,128)}, f32[256,256]{1,0:T(8,128)}) custom-call(f32[256,256]{1,0:T(8,128)} %shard_map.74.part_ref, f32[256,256]{1,0:T(8,128)} %convolution_bitcast_fusion.1.test_gram_ref, f32[256,256]{1,0:T(8,128)} %convolution_bitcast_fusion.build_gram_ref), custom_call_target="tpu_custom_call" | custom-call | tf_op jit(solution)/shard_map/pallas_call | solution.py:267
  77.2 1.8 %convolution_bitcast_fusion.2 = f32[1,16,256]{2,1,0:T(8,128)} fusion(f32[16,256]{1,0:T(8,128)} %get-tuple-element.11, f32[256,256]{1,0:T(8,128)} %get-tuple-element.12), kind=kOutput, calls=%fused_computation.2 | convolution fusion | flops 12582912 | bytes 294912 | tf_op jit(solution)/shard_map/dot_general | solution.py:367
Async XLA Ops:
  25.3 11.1 %copy-start = (bf16[8,16,6,256]{3,2,1,0:T(8,128)(2,1)S(1)}, bf16[8,16,6,256]{3,2,1,0:T(8,128)(2,1)}, u32[]{:S(2)}) copy-start(bf16[8,16,6,256]{3,2,1,0:T(8,128)(2,1)} %get-tuple-element.10) | copy-start | bytes 1179652
  25.3 12.1 %copy-start.1 = (bf16[2,16,16,256]{3,2,1,0:T(8,128)(2,1)S(1)}, bf16[2,16,16,256]{3,2,1,0:T(8,128)(2,1)}, u32[]{:S(2)}) copy-start(bf16[2,16,16,256]{3,2,1,0:T(8,128)(2,1)} %get-tuple-element.9) | copy-start | bytes 786436

commit v17 on v16

--- a/solution.py
+++ b/solution.py
@@ -146,7 +146,7 @@
         a_ref[pl.ds(k, 1), :] = jnp.where(is_k, -inv, row * inv)
         return next_row
 
-    lax.fori_loop(0, n, step, a_ref[0:1, :], unroll=128)
+    lax.fori_loop(0, n, step, a_ref[0:1, :], unroll=256)
     a_ref[...] = -a_ref[...]
 
 

time: 79.6 us -> 79.1 us (level)
    pallas_call x1, Pallas kernels: 8.43 us -> 4.99 us  [local_mttkrp(): pl.pallas_call(functools.partial(mttkrp_kernel, CHUNK, n_test_blocks, SB)...]
    pallas_call x1, Pallas kernels: 38.8 us -> 42.1 us  [exchange_and_invert(): pl.pallas_call(functools.partial(tail_kernel, n_build, n_test), out_shape...]
where the time goes in v17:
time: 79.1 us; the launch traced here: 78.8 us
  Pallas kernels  72.4 us (92%)
  matrix products  3.77 us (5%)
  local copies, waits for them, and re-layouts  2 us (3%)
    pallas_call x1, Pallas kernels, exchange_and_invert(): pl.pallas_call(functools.partial(tail_kernel, n_build, n_test), out_shape...  42.1 us
    pallas_call x1, Pallas kernels, gather_factors(): pl.pallas_call(functools.partial(gather_kernel, n_build, n_test, n_stmt),...  25.3 us
    pallas_call x1, Pallas kernels, local_mttkrp(): pl.pallas_call(functools.partial(mttkrp_kernel, CHUNK, n_test_blocks, SB)...  4.99 us
    reshape x1, local copies, waits for them, and re-layouts, gather_factors(): build_pieces.reshape(-1, build_rows.shape[-1])  1.99 us
    dot_general x1, matrix products, shards(): jnp.dot(owned_sums, inverse, precision=lax.Precision.HIGHEST, preferred_e...  1.8 us

profile of v17, /device:TPU:1, one launch (start us, length us, event | category | flops | bytes accessed | tf_op | source)
XLA Modules:
  0.0 78.8 jit_solution(5213673917488772825)
XLA Ops:
  0.0 25.3 %shard_map.73 = (bf16[2,16,16,256]{3,2,1,0:T(8,128)(2,1)}, bf16[8,16,6,256]{3,2,1,0:T(8,128)(2,1)}) custom-call(bf16[16,256]{1,0:T(8,128)(2,1)} %bitcast.25, bf16[6,256]{1,0:T(8,128)(2,1)} %bitcast.26), custom_call_target="tpu_custom_call" | custom-call | tf_op jit(solution)/shard_map/pallas_call | solution.py:107
  25.3 0.0 copy-start
  25.3 0.0 copy-start.1
  25.3 2.0 %reshape.7.build_ref = bf16[768,256]{1,0:T(8,128)(2,1)} reshape(bf16[8,16,6,256]{3,2,1,0:T(8,128)(2,1)} %get-tuple-element.10) | data formatting | bytes 786432 | tf_op jit(solution)/shard_map/reshape | solution.py:126
  28.0 5.0 %shard_map.74.part_ref = f32[256,256]{1,0:T(8,128)} custom-call(s32[2]{0:T(128)} %bitcast.27, s32[2]{0:T(128)} %bitcast.28, s32[2]{0:T(128)} %bitcast.29, s32[1]{0:T(128)} %bitcast.22.live_count, bf16[512,256]{1,0:T(8,128)(2,1)} %bitcast.24, bf16[768,256]{1,0:T(8,128)(2,1)} %reshape.7.build_ref, bf16[2,128,128,128]{3,2,1,0:T(8,128)(2,1)} %bitcast.23), custom_call_target="tpu_custom_call" | custom-call | tf_op jit(solution)/shard_map/pallas_call | solution.py:351
  33.0 0.0 copy-done
  33.0 1.0 %convolution_bitcast_fusion.build_gram_ref = f32[256,256]{1,0:T(8,128)} fusion(bf16[8,16,6,256]{3,2,1,0:T(8,128)(2,1)S(1)} %copy-done), kind=kOutput, calls=%fused_computation | convolution fusion | flops 100663296 | bytes 655360 | tf_op jit(solution)/shard_map/dot_general | solution.py:365
  34.0 0.0 copy-done.1
  34.0 1.0 %convolution_bitcast_fusion.1.test_gram_ref = f32[256,256]{1,0:T(8,128)} fusion(bf16[2,16,16,256]{3,2,1,0:T(8,128)(2,1)S(1)} %copy-done.1), kind=kOutput, calls=%fused_computation.1 | convolution fusion | flops 67108864 | bytes 524288 | tf_op jit(solution)/shard_map/dot_general | solution.py:364
  34.9 42.1 %shard_map.75 = (f32[16,256]{1,0:T(8,128)}, f32[256,256]{1,0:T(8,128)}) custom-call(f32[256,256]{1,0:T(8,128)} %shard_map.74.part_ref, f32[256,256]{1,0:T(8,128)} %convolution_bitcast_fusion.1.test_gram_ref, f32[256,256]{1,0:T(8,128)} %convolution_bitcast_fusion.build_gram_ref), custom_call_target="tpu_custom_call" | custom-call | tf_op jit(solution)/shard_map/pallas_call | solution.py:267
  77.0 1.8 %convolution_bitcast_fusion.2 = f32[1,16,256]{2,1,0:T(8,128)} fusion(f32[16,256]{1,0:T(8,128)} %get-tuple-element.11, f32[256,256]{1,0:T(8,128)} %get-tuple-element.12), kind=kOutput, calls=%fused_computation.2 | convolution fusion | flops 12582912 | bytes 294912 | tf_op jit(solution)/shard_map/dot_general | solution.py:367
Async XLA Ops:
  25.3 7.7 %copy-start = (bf16[8,16,6,256]{3,2,1,0:T(8,128)(2,1)S(1)}, bf16[8,16,6,256]{3,2,1,0:T(8,128)(2,1)}, u32[]{:S(2)}) copy-start(bf16[8,16,6,256]{3,2,1,0:T(8,128)(2,1)} %get-tuple-element.10) | copy-start | bytes 1179652
  25.3 8.7 %copy-start.1 = (bf16[2,16,16,256]{3,2,1,0:T(8,128)(2,1)S(1)}, bf16[2,16,16,256]{3,2,1,0:T(8,128)(2,1)}, u32[]{:S(2)}) copy-start(bf16[2,16,16,256]{3,2,1,0:T(8,128)(2,1)} %get-tuple-element.9) | copy-start | bytes 786436
